TPU v7x, 256 devices: a whole 4x4x8 slice. The times are simulated.
256 devices in a mesh: dp: 64 (over x, y, z_hi, core), mp: 4 (over z_lo).
Axes of the slice: x: 4, y: 4, z: 8 (z_hi: 2, z_lo: 4; z = z_hi * 4 + z_lo), core: 2. Of those that a mesh axis runs over, the one named last changes fastest.
Arguments:
- hidden: bfloat16 [32768, 16384], P('dp', 'mp'), may hold values from -64 to 64
- key_weight: bfloat16 [16384, 1024], P(('mp', 'dp')), may hold values from -0.046875 to 0.046875
- key_state: float32 [16384], P(('mp', 'dp')), may hold values from 2.9802323e-09 to 1.1920929e-07
- key_cotangent: bfloat16 [32768, 1024], P('dp'), may hold values from -6 to 6
- doc_lengths: int32 [128, 4], P('dp'), may hold values from 1 to 128, 256 in all within a row
Outputs:
- input_grad: bfloat16 [32768, 16384], P('dp', 'mp')
- new_weight: bfloat16 [16384, 1024], P(('mp', 'dp'))
- new_state: float32 [16384], P(('mp', 'dp'))
Inputs may be any that keep to these rules, and one draw needn't show every extreme that they name: `doc_lengths`: each row lists the lengths of the documents of one sequence, in order, summing to 256.
All inputs are finite; a program needn't handle non-finite values.
Results may differ from a plain program's by a relative error of at most 0.0045.
Values may be sent and summed in bfloat16 or wider, within the bound.
No kernel may reach another device: no remote copies, remote signals or barrier semaphores. Data moves between devices by JAX's collectives and lax.ppermute only.
A program may use at most 128 MiB of HBM per device.

v0:
```python
import functools

import jax
import jax.numpy as jnp
from jax import lax
from jax.experimental import pallas as pl
from jax.experimental.pallas import tpu as pltpu
from jax.sharding import Mesh
from jax.sharding import PartitionSpec as P

HD = 128
LEN = 256
KVW = 1024
HALF = 512
DP = ("x", "y", "zh", "c")
MP_DP = ("mp", "x", "y", "zh", "c")
RATE = 0.01
BF = jnp.bfloat16
F32 = jnp.float32
VM = pl.BlockSpec(memory_space=pltpu.VMEM)
SM = pl.BlockSpec(memory_space=pltpu.SMEM)
ANY = pl.BlockSpec(memory_space=pl.ANY)
MIB = 1 << 20


def call(body, outs, in_specs, out_specs=None, scratch=(), vmem=8, flops=0, moved=0, alias=None):
    return pl.pallas_call(
        body,
        out_shape=outs,
        in_specs=in_specs,
        out_specs=[VM] * len(outs) if out_specs is None else out_specs,
        scratch_shapes=list(scratch),
        input_output_aliases=alias or {},
        compiler_params=pltpu.CompilerParams(vmem_limit_bytes=vmem * MIB),
        cost_estimate=pl.CostEstimate(flops=flops, bytes_accessed=moved, transcendentals=0),
    )


def struct(shape, dtype):
    return jax.ShapeDtypeStruct(shape, dtype)


def spread(value, by):
    pairs = []
    for x in range(4):
        for y in range(4):
            here = (4 * x + y) * 2
            pairs.append((here, (4 * ((x + by) % 4) + y) * 2))
            pairs.append((here + 1, (4 * x + (y + by) % 4) * 2 + 1))
    return lax.ppermute(value, ("x", "y", "c"), pairs)


def spread_across(value, by):
    pairs = []
    for x in range(4):
        for y in range(4):
            here = (4 * x + y) * 2
            pairs.append((here, (4 * x + (y + by) % 4) * 2))
            pairs.append((here + 1, (4 * ((x + by) % 4) + y) * 2 + 1))
    return lax.ppermute(value, ("x", "y", "c"), pairs)


def swap_cores(value):
    return lax.ppermute(value, "c", [(0, 1), (1, 0)])


def rope_kernel(len_ref, cot_ref, grad_ref, turned_ref):
    lane = lax.broadcasted_iota(jnp.int32, (LEN, HD), 1)
    place = lax.broadcasted_iota(jnp.int32, (LEN, HD), 0)
    index = jnp.where(lane < HD // 2, lane, lane - HD // 2).astype(F32)
    frequency = jnp.exp(-(2.0 * index / HD) * jnp.log(jnp.full((LEN, HD), 500000.0, F32)))
    row = lax.broadcasted_iota(jnp.int32, (HD, HD), 0)
    col = lax.broadcasted_iota(jnp.int32, (HD, HD), 1)
    eye = (row == col).astype(F32).astype(BF)
    far = jnp.where(col < HD // 2, col + HD // 2, col - HD // 2)
    swap = (row == far).astype(F32).astype(BF)
    for seq in range(2):
        start = jnp.int32(0)
        first = jnp.zeros((LEN, HD), jnp.int32)
        for doc in range(1, 4):
            start = start + len_ref[seq, doc - 1]
            first = jnp.where(place >= start, start, first)
        angle = (place - first).astype(F32) * frequency
        cos = jnp.cos(angle)
        sin = jnp.sin(angle)
        sin = jnp.where(lane < HD // 2, sin, -sin)
        rows = pl.ds(seq * LEN, LEN)
        for head in range(KVW // HD):
            cols = pl.ds(head * HD, HD)
            value = cot_ref[rows, cols]
            swapped = jnp.dot(value, swap, preferred_element_type=F32)
            out = (value.astype(F32) * cos + swapped * sin).astype(BF)
            grad_ref[rows, cols] = out
            turned = lax.dot_general(
                eye, out, (((1,), (1,)), ((), ())), preferred_element_type=F32
            )
            turned_ref[cols, rows] = turned.astype(BF)


def rope(doc_lengths, cotangent):
    return call(
        rope_kernel,
        [struct((512, KVW), BF), struct((KVW, 512), BF)],
        [SM, VM],
        vmem=12,
        moved=3 * MIB,
    )(doc_lengths, cotangent)


def split_kernel(at_ref, hidden_ref, mine, other):
    core = at_ref[2]
    for j in range(16):
        here = pl.ds(j * 128, 128)
        mine[:, here] = hidden_ref[:, pl.ds(pl.multiple_of((2 * j + core) * 128, 128), 128)]
        other[:, here] = hidden_ref[:, pl.ds(pl.multiple_of((2 * j + 1 - core) * 128, 128), 128)]


def split(at, hidden):
    half = pl.BlockSpec((256, 2048), lambda i: (i, 0))
    return pl.pallas_call(
        split_kernel,
        grid=(2,),
        in_specs=[SM, pl.BlockSpec((256, 4096), lambda i: (i, 0))],
        out_specs=[half, half],
        out_shape=[struct((512, 2048), BF)] * 2,
        compiler_params=pltpu.CompilerParams(vmem_limit_bytes=16 * MIB),
        cost_estimate=pl.CostEstimate(flops=0, bytes_accessed=8 * MIB, transcendentals=0),
    )(at, hidden)


def tile(at_ref, first, second):
    core = at_ref[2]
    return first * jnp.where(core == 0, 4, 1) + second * jnp.where(core == 0, 1, 4)


def grad_kernel(steps, at_ref, own_t, other_t, mine, other_h, *outs):
    first = at_ref[0]
    for j, out in zip(steps, outs):
        to = lax.rem(first + j, 4)
        tiles = [pl.ds(pl.multiple_of(tile(at_ref, to, i) * 128, 128), 128) for i in range(4)]
        for half in (0, 1):
            pair = tiles[2 * half : 2 * half + 2]
            right = jnp.concatenate(
                [jnp.concatenate([h[:, t] for t in pair], axis=1) for h in (mine, other_h)],
                axis=0,
            )
            for part in (0, 1):
                rows = slice(part * HALF, part * HALF + HALF)
                left = jnp.concatenate([own_t[rows, :], other_t[rows, :]], axis=1)
                value = jnp.dot(left, right, preferred_element_type=F32)
                out[rows, half * 256 : half * 256 + 256] = value.astype(out.dtype)


def grad_parts(steps, at, own_t, other_t, mine, other_h):
    outs = [struct((KVW, 512), BF if j else F32) for j in steps]
    return call(
        functools.partial(grad_kernel, steps),
        outs,
        [SM, VM, VM, VM, VM],
        vmem=20,
        flops=2 * 1024 * 512 * 1024 * len(steps),
        moved=8 * MIB,
    )(at, own_t, other_t, mine, other_h)


def first_sum_kernel(at_ref, *refs):
    held, outs = refs[:4], refs[4:]
    for j in range(4):
        cols = pl.ds(pl.multiple_of(lax.rem(at_ref[1] + j, 4) * 128, 128), 128)
        total = held[0][:, cols]
        for ref in held[1:]:
            total += ref[:, cols].astype(F32)
        outs[j][...] = total.astype(outs[j].dtype)


def first_sum(at, parts):
    kinds = [struct((KVW, 128), F32)] + [struct((KVW, 128), BF)] * 3
    return call(first_sum_kernel, kinds, [SM] + [VM] * 4, vmem=14, moved=6 * MIB)(at, *parts)


def second_sum_kernel(at_ref, *refs):
    held = refs[:4]
    q_out, p_out, local_out, full = refs[4:]
    zh, core = at_ref[3], at_ref[2]
    total = held[0][...]
    for ref in held[1:]:
        total += ref[...].astype(F32)
    full[...] = total.T
    mine = full[pl.ds(pl.multiple_of(core * 64, 64), 64), :]
    other = full[pl.ds(pl.multiple_of((1 - core) * 64, 64), 64), :]
    straight = zh == core
    q_out[...] = jnp.where(straight, other, mine).astype(BF)
    p_out[...] = other.astype(BF)
    local_out[...] = jnp.where(straight, mine, 0.0)


def second_sum(at, parts):
    return call(
        second_sum_kernel,
        [struct((64, KVW), BF), struct((64, KVW), BF), struct((64, KVW), F32)],
        [SM] + [VM] * 4,
        scratch=[pltpu.VMEM((128, KVW), F32)],
        moved=2 * MIB,
    )(at, *parts)


def third_sum_kernel(local, q_in, p_in, grad_out, rows_out, total_out):
    grad = local[...] + (q_in[...].astype(F32) + p_in[...].astype(F32))
    grad_out[...] = grad
    rows = jnp.sum(grad * grad, axis=1, keepdims=True)
    rows_out[...] = jnp.broadcast_to(rows, (64, 128))
    total = jnp.sum(rows, axis=0, keepdims=True)
    total_out[...] = jnp.broadcast_to(total, (8, 128))


def third_sum(local, q_in, p_in):
    return call(
        third_sum_kernel,
        [struct((64, KVW), F32), struct((64, 128), F32), struct((8, 128), F32)],
        [VM] * 3,
        moved=MIB,
    )(local, q_in, p_in)


def send_all(value, axes):
    copies = jnp.broadcast_to(value[None], (lax.axis_size(axes), *value.shape))
    return lax.all_to_all(copies, axes, 0, 0, tiled=True)


def spread_sum(value, axes):
    return jnp.sum(send_all(value, axes), axis=0)


def update_kernel(total, rows, grad, weight, state, weight_out, state_out):
    squares = total[0:1, 0:1]
    clip = jnp.minimum(1.0, 1.0 / jnp.sqrt(squares + 1e-06))
    row = lax.broadcasted_iota(jnp.int32, (64, 64), 0)
    col = lax.broadcasted_iota(jnp.int32, (64, 64), 1)
    eye = row == col
    held = jnp.sum(jnp.where(eye, state[...], 0.0), axis=1, keepdims=True)
    new = held + clip * clip * (rows[:, 0:1] * (1.0 / KVW))
    state_out[...] = jnp.sum(jnp.where(eye, new, 0.0), axis=0, keepdims=True)
    step = RATE * clip * grad[...] / (jnp.sqrt(new) + 1e-10)
    weight_out[...] = (weight[...].astype(F32) - step).astype(BF)


def update(total, rows, grad, weight, state):
    new_weight, new_state = call(
        update_kernel,
        [struct((64, KVW), BF), struct((1, 64), F32)],
        [VM] * 5,
        moved=MIB,
    )(total, rows, grad, weight, state.reshape(1, 64))
    return new_weight, new_state.reshape(64)


def input_kernel(at_ref, grad_ref, *refs):
    own, far = refs[:4], refs[4:8]
    out, held, sem = refs[8:]
    first, second, core = at_ref[0], at_ref[1], at_ref[2]
    order = sorted(((k, j) for k in range(4) for j in range(4)), key=lambda t: (max(t), t))
    copies = []
    for n, (k, j) in enumerate(order):
        weight = jnp.concatenate([own[k][j], far[j][k]], axis=0)
        value = lax.dot_general(
            grad_ref[...], weight, (((1,), (1,)), ((), ())), preferred_element_type=F32
        ).astype(BF)
        row = tile(at_ref, lax.rem(first + 4 - j, 4), lax.rem(second + 4 - k, 4))
        for i, side in enumerate((core, 1 - core)):
            held[n, i] = value[:, i * 128 : i * 128 + 128]
            cols = pl.ds(pl.multiple_of((2 * row + side) * 128, 128), 128)
            copy = pltpu.make_async_copy(held.at[n, i], out.at[:, cols], sem.at[2 * n + i])
            copy.start()
            copies.append(copy)
    for copy in copies:
        copy.wait()


def input_product(at, key_grad, own, far):
    return call(
        input_kernel,
        [struct((512, 4096), BF)],
        [SM] + [VM] * 9,
        out_specs=[ANY],
        scratch=[pltpu.VMEM((16, 2, 512, 128), BF), pltpu.SemaphoreType.DMA((32,))],
        vmem=22,
        flops=2 * 512 * 1024 * 4096,
        moved=13 * MIB,
    )(at, key_grad, *own, *far)[0]


def shards(hidden, key_weight, key_state, key_cotangent, doc_lengths):
    x, y, zh, core = (lax.axis_index(name) for name in DP)
    first = jnp.where(core == 0, x, y)
    second = jnp.where(core == 0, y, x)
    at = jnp.stack([first, second, core, zh]).astype(jnp.int32)
    straight = zh == core

    mine, other_h = split(at, hidden)
    other_h = swap_cores(other_h)
    key_grad, turned = rope(doc_lengths, key_cotangent)
    other_t = swap_cores(turned)

    part2, part1 = grad_parts((2, 1), at, turned, other_t, mine, other_h)
    part3, part0 = grad_parts((3, 0), at, turned, other_t, mine, other_h)
    parts = [part0] + [spread(v, j) for j, v in ((1, part1), (2, part2), (3, part3))]

    weight, _ = lax.optimization_barrier((key_weight, part0))
    q_w = lax.ppermute(weight, ("zh", "c"), [(0, 2), (1, 0), (2, 3), (3, 1)])
    p_w = lax.ppermute(weight, ("zh", "c"), [(1, 2), (2, 1)])
    same = jnp.where(straight, key_weight, q_w)
    cross = jnp.where(straight, q_w, p_w)
    rows = jnp.concatenate(
        [jnp.where(core == 0, same, cross), jnp.where(core == 0, cross, same)], axis=0
    )

    near = [spread(rows, 1), spread(rows, 3)]
    parts[0], rows, *near = lax.optimization_barrier((parts[0], rows, *near))

    sums = first_sum(at, parts)
    ring = [rows, near[0], spread(rows, 2), near[1]]
    sums = [sums[0]] + [spread_across(sums[j], j) for j in (1, 2, 3)]
    q_out, p_out, local = second_sum(at, sums)
    q_in = lax.ppermute(q_out, ("zh", "c"), [(0, 1), (1, 3), (2, 0), (3, 2)])
    p_in = lax.ppermute(p_out, ("zh", "c"), [(2, 1), (1, 2)])

    *ring, _ = lax.optimization_barrier((*ring, q_out))
    cat = jnp.stack(ring)
    own = [cat] + [spread_across(cat, j) for j in (1, 2, 3)]

    grad, squares, total = third_sum(local, q_in, p_in)
    far = [swap_cores(cat)]
    total = lax.psum(total, "c")
    total = spread_sum(total, ("zh", "mp"))
    *rest, total = lax.optimization_barrier((*own[1:], total))
    far += [swap_cores(v) for v in rest]
    own = [cat, *rest]
    everywhere = send_all(total, ("x", "y"))
    input_grad = input_product(at, key_grad, own, far)
    input_grad, everywhere = lax.optimization_barrier((input_grad, everywhere))
    total = jnp.sum(everywhere, axis=0)
    new_weight, new_state = update(total, squares, grad, key_weight, key_state)
    return (input_grad, new_weight, new_state)


def solution(mesh):
    finer = Mesh(mesh.devices.reshape(4, 4, 2, 2, mesh.shape["mp"]), (*DP, "mp"))
    placed = (P(DP, "mp"), P(MP_DP, None), P(MP_DP), P(DP, None), P(DP, None))
    return jax.shard_map(
        shards,
        mesh=finer,
        in_specs=placed,
        out_specs=(P(DP, "mp"), P(MP_DP, None), P(MP_DP)),
        check_vma=False,
    )
```

profile of v0, /device:TPU:1, one launch (start us, length us, event | category | flops | bytes accessed | tf_op | source)
XLA Modules:
  0.0 118.0 jit_solution(5233757513365501879)
XLA Ops:
  0.6 0.1 pad_add_fusion.at_ref
  0.7 2.2 %copy-done = bf16[512,4096]{1,0:T(8,128)(2,1)S(1)} copy-done((bf16[512,4096]{1,0:T(8,128)(2,1)S(1)}, bf16[512,4096]{1,0:T(8,128)(2,1)}, u32[]{:S(2)}) %copy-start) | copy-done | bytes 4194328
  2.9 1.7 %shard_map.77 = (bf16[512,2048]{1,0:T(8,128)(2,1)S(1)}, bf16[512,2048]{1,0:T(8,128)(2,1)S(1)}) custom-call(s32[4]{0:T(128)S(1)} %pad_add_fusion.at_ref, bf16[512,4096]{1,0:T(8,128)(2,1)S(1)} %copy-done), custom_call_target="tpu_custom_call" | custom-call | bytes 8388608 | tf_op jit(solution)/shard_map/pallas_call | solution.py:120
  4.6 3.3 %collective-permute-start.1 = (bf16[512,2048]{1,0:T(8,128)(2,1)S(1)}, bf16[512,2048]{1,0:T(8,128)(2,1)S(1)}, u32[]{:S(2)}, u32[]{:S(2)}) collective-permute-start(bf16[512,2048]{1,0:T(8,128)(2,1)S(1)} %get-tuple-element.41), channel_id=1, source_target_pairs={{0,4},{4,0},{1,5},{5,1},{2,6},{6,2},{3,7},{7,3},{8,12},{12,8},{9,1... | collective-permute-start | bytes 6291464 | tf_op jit(solution)/shard_map/ppermute | solution.py:64
  8.0 2.5 %shard_map.76 = (bf16[512,1024]{1,0:T(8,128)(2,1)S(1)}, bf16[1024,512]{1,0:T(8,128)(2,1)S(1)}) custom-call(s32[2,4]{1,0:T(2,128)S(1)} %copy-done.3, bf16[512,1024]{1,0:T(8,128)(2,1)S(1)} %copy-done.1), custom_call_target="tpu_custom_call" | custom-call | bytes 3145728 | tf_op jit(solution)/shard_map/pallas_call | solution.py:101
  10.5 1.0 copy-done.5
  11.5 2.6 %collective-permute-done.other_t = bf16[1024,512]{1,0:T(8,128)(2,1)S(1)} collective-permute-done((bf16[1024,512]{1,0:T(8,128)(2,1)S(1)}, bf16[1024,512]{1,0:T(8,128)(2,1)S(1)}, u32[]{:S(2)}, u32[]{:S(2)}) %collective-permute-start) | collective-permute-done | bytes 1048608 | tf_op jit(solution)/shard_map/ppermute | solution.py:64
  14.1 4.1 %shard_map.79 = (bf16[1024,512]{1,0:T(8,128)(2,1)}, bf16[1024,512]{1,0:T(8,128)(2,1)}) custom-call(s32[4]{0:T(128)S(1)} %pad_add_fusion.at_ref, bf16[1024,512]{1,0:T(8,128)(2,1)S(1)} %get-tuple-element.39.own_t, bf16[1024,512]{1,0:T(8,128)(2,1)S(1)} %collective-permute-done.other_t, bf16[512,2048]{1,0:T(8,128)(2,1)S(1)} %get-tuple-element.40.mine, ...), custom_call_target="tpu_custom_call" | custom-call | flops 2147483648 | bytes 8388608 | tf_op jit(solution)/shard_map/pallas_call | solution.py:156
  18.3 2.2 %collective-permute-start.8 = (bf16[1024,512]{1,0:T(8,128)(2,1)}, bf16[1024,512]{1,0:T(8,128)(2,1)}, u32[]{:S(2)}, u32[]{:S(2)}) collective-permute-start(bf16[1024,512]{1,0:T(8,128)(2,1)} %get-tuple-element.49), channel_id=1, source_target_pairs={{0,128},{4,36},{16,144},{20,52},{32,160},{36,4},{48,176},{52,20},{... | collective-permute-start | bytes 3145736 | tf_op jit(solution)/shard_map/ppermute | solution.py:50
  20.4 3.3 %shard_map.78 = (bf16[1024,512]{1,0:T(8,128)(2,1)}, f32[1024,512]{1,0:T(8,128)S(1)}) custom-call(s32[4]{0:T(128)S(1)} %pad_add_fusion.at_ref, bf16[1024,512]{1,0:T(8,128)(2,1)S(1)} %get-tuple-element.39.own_t, bf16[1024,512]{1,0:T(8,128)(2,1)S(1)} %collective-permute-done.other_t, bf16[512,2048]{1,0:T(8,128)(2,1)S(1)} %get-tuple-element.40.mine, ...), custom_call_target="tpu_custom_call" | custom-call | flops 2147483648 | bytes 8388608 | tf_op jit(solution)/shard_map/pallas_call | solution.py:156
  23.8 1.0 collective-permute-start.9
  24.8 0.8 collective-permute-start.2
  25.6 8.7 %collective-permute-start.3 = (bf16[64,1024]{1,0:T(8,128)(2,1)S(1)}, bf16[64,1024]{1,0:T(8,128)(2,1)S(1)}, u32[]{:S(2)}, u32[]{:S(2)}) collective-permute-start(bf16[64,1024]{1,0:T(8,128)(2,1)S(1)} %copy-done.2), channel_id=1, source_target_pairs={{4,8},{8,4},{5,9},{9,5},{6,10},{10,6},{7,11},{11,7},{20,24},{24,20... | collective-permute-start | bytes 393224 | tf_op jit(solution)/shard_map/ppermute | solution.py:310
  34.4 4.0 %collective-permute-done.3 = bf16[64,1024]{1,0:T(8,128)(2,1)S(1)} collective-permute-done((bf16[64,1024]{1,0:T(8,128)(2,1)S(1)}, bf16[64,1024]{1,0:T(8,128)(2,1)S(1)}, u32[]{:S(2)}, u32[]{:S(2)}) %collective-permute-start.3) | collective-permute-done | bytes 131104 | tf_op jit(solution)/shard_map/ppermute | solution.py:310
  38.4 0.8 collective-permute-start.4
  39.2 2.0 %collective-permute-start.5 = (bf16[128,1024]{1,0:T(8,128)(2,1)S(1)}, bf16[128,1024]{1,0:T(8,128)(2,1)S(1)}, u32[]{:S(2)}, u32[]{:S(2)}) collective-permute-start(bf16[128,1024]{1,0:T(8,128)(2,1)S(1)} %pad_maximum_fusion.1), channel_id=1, source_target_pairs={{0,192},{4,52},{16,208},{20,4},{32,224},{36,20},{48,240},{52,36},{... | collective-permute-start | bytes 786440 | tf_op jit(solution)/shard_map/ppermute | solution.py:50
  41.2 6.5 %collective-permute-done.4 = bf16[128,1024]{1,0:T(8,128)(2,1)S(1)} collective-permute-done((bf16[128,1024]{1,0:T(8,128)(2,1)S(1)}, bf16[128,1024]{1,0:T(8,128)(2,1)S(1)}, u32[]{:S(2)}, u32[]{:S(2)}) %collective-permute-start.4) | collective-permute-done | bytes 262176 | tf_op jit(solution)/shard_map/ppermute | solution.py:50
  47.7 0.6 collective-permute-done.5
  48.3 2.2 %shard_map.80 = (f32[1024,128]{1,0:T(8,128)S(1)}, bf16[1024,128]{1,0:T(8,128)(2,1)S(1)}, bf16[1024,128]{1,0:T(8,128)(2,1)S(1)}, bf16[1024,128]{1,0:T(8,128)(2,1)S(1)}) custom-call(s32[4]{0:T(128)S(1)} %pad_add_fusion.at_ref, f32[1024,512]{1,0:T(8,128)S(1)} %get-tuple-element.47.refs_0_, bf16[1024,512]{1,0:T(8,128)(2,1)S(1)} %collective-permute-done.7.refs_1_, ...), custom_call_target="tpu_custom_call" | custom-call | bytes 6291456 | tf_op jit(solution)/shard_map/pallas_call | solution.py:178
  50.5 0.1 collective-permute-start.10
  50.6 2.6 %collective-permute-start.11 = (bf16[1024,128]{1,0:T(8,128)(2,1)S(1)}, bf16[1024,128]{1,0:T(8,128)(2,1)S(1)}, u32[]{:S(2)}, u32[]{:S(2)}) collective-permute-start(bf16[1024,128]{1,0:T(8,128)(2,1)S(1)} %get-tuple-element.53), channel_id=1, source_target_pairs={{0,32},{4,132},{16,48},{20,148},{32,0},{36,164},{48,16},{52,180},{... | collective-permute-start | bytes 786440 | tf_op jit(solution)/shard_map/ppermute | solution.py:60
  53.2 0.9 collective-permute-start.12
  54.0 2.5 %collective-permute-start.6 = (bf16[128,1024]{1,0:T(8,128)(2,1)S(1)}, bf16[128,1024]{1,0:T(8,128)(2,1)S(1)}, u32[]{:S(2)}, u32[]{:S(2)}) collective-permute-start(bf16[128,1024]{1,0:T(8,128)(2,1)S(1)} %pad_maximum_fusion.1), channel_id=1, source_target_pairs={{0,128},{4,36},{16,144},{20,52},{32,160},{36,4},{48,176},{52,20},{... | collective-permute-start | bytes 786440 | tf_op jit(solution)/shard_map/ppermute | solution.py:50
  56.6 3.6 %collective-permute-done.10.refs_1_ = bf16[1024,128]{1,0:T(8,128)(2,1)S(1)} collective-permute-done((bf16[1024,128]{1,0:T(8,128)(2,1)S(1)}, bf16[1024,128]{1,0:T(8,128)(2,1)S(1)}, u32[]{:S(2)}, u32[]{:S(2)}) %collective-permute-start.10) | collective-permute-done | bytes 262176 | tf_op jit(solution)/shard_map/ppermute | solution.py:60
  60.1 0.7 collective-permute-done.12.refs_3_
  60.9 0.8 shard_map.81
  61.7 2.3 %collective-permute-done.6 = bf16[128,1024]{1,0:T(8,128)(2,1)S(1)} collective-permute-done((bf16[128,1024]{1,0:T(8,128)(2,1)S(1)}, bf16[128,1024]{1,0:T(8,128)(2,1)S(1)}, u32[]{:S(2)}, u32[]{:S(2)}) %collective-permute-start.6) | collective-permute-done | bytes 262176 | tf_op jit(solution)/shard_map/ppermute | solution.py:50
  64.0 0.1 pad_maximum_fusion.refs_0_
  64.1 0.6 collective-permute-start.13
  64.7 1.2 collective-permute-start.14
  65.8 2.0 %collective-permute-start.15 = (bf16[4,128,1024]{2,1,0:T(8,128)(2,1)S(1)}, bf16[4,128,1024]{2,1,0:T(8,128)(2,1)}, u32[]{:S(2)}, u32[]{:S(2)}) collective-permute-start(bf16[4,128,1024]{2,1,0:T(8,128)(2,1)S(1)} %pad_maximum_fusion.refs_0_), channel_id=1, source_target_pairs={{0,48},{4,196},{16,0},{20,212},{32,16},{36,228},{48,32},{52,244},{... | collective-permute-start | bytes 3145736 | tf_op jit(solution)/shard_map/ppermute | solution.py:60
  67.8 5.7 %collective-permute-start.16 = (bf16[64,1024]{1,0:T(8,128)(2,1)S(1)}, bf16[64,1024]{1,0:T(8,128)(2,1)S(1)}, u32[]{:S(2)}, u32[]{:S(2)}) collective-permute-start(bf16[64,1024]{1,0:T(8,128)(2,1)S(1)} %get-tuple-element.55), channel_id=1, source_target_pairs={{0,4},{4,12},{8,0},{12,8},{1,5},{5,13},{9,1},{13,9},{2,6},{6,14},{... | collective-permute-start | bytes 393224 | tf_op jit(solution)/shard_map/ppermute | solution.py:324
  73.5 6.4 %collective-permute-start.17 = (bf16[64,1024]{1,0:T(8,128)(2,1)S(1)}, bf16[64,1024]{1,0:T(8,128)(2,1)S(1)}, u32[]{:S(2)}, u32[]{:S(2)}) collective-permute-start(bf16[64,1024]{1,0:T(8,128)(2,1)S(1)} %get-tuple-element.61), channel_id=1, source_target_pairs={{8,4},{4,8},{9,5},{5,9},{10,6},{6,10},{11,7},{7,11},{24,20},{20,24... | collective-permute-start | bytes 393224 | tf_op jit(solution)/shard_map/ppermute | solution.py:325
  79.9 3.8 %collective-permute-done.17.p_in = bf16[64,1024]{1,0:T(8,128)(2,1)S(1)} collective-permute-done((bf16[64,1024]{1,0:T(8,128)(2,1)S(1)}, bf16[64,1024]{1,0:T(8,128)(2,1)S(1)}, u32[]{:S(2)}, u32[]{:S(2)}) %collective-permute-start.17) | collective-permute-done | bytes 131104 | tf_op jit(solution)/shard_map/ppermute | solution.py:325
  83.8 0.1 shard_map.82
  83.9 2.5 %psum.7 = f32[8,128]{1,0:T(8,128)S(1)} all-reduce(f32[8,128]{1,0:T(8,128)S(1)} %get-tuple-element.62), channel_id=1, replica_groups=mesh['x'=4,'y'=4,'zh'=2,'c'=2,'mp'=4] {'c'}, use_global_device_ids=true, to_apply=%region_0.1 | all-reduce | flops 1024 | bytes 8192 | tf_op jit(solution)/shard_map/psum | solution.py:333
  86.4 0.6 broadcast_in_dim.4
  87.0 6.7 %all-to-all-start = ((f32[8,8,128]{2,1,0:T(8,128)}), f32[8,8,128]{2,1,0:T(8,128)S(1)}, u32[]{:S(2)}, u32[]{:S(2)}) async-start(f32[8,8,128]{2,1,0:T(8,128)} %broadcast_in_dim.4), calls=%async_computation | async-start | bytes 65536 | tf_op jit(solution)/shard_map/all_to_all | solution.py:227
  93.7 0.6 collective-permute-start.18
  94.3 6.3 %all-to-all-done = f32[8,8,128]{2,1,0:T(8,128)S(1)} async-done(((f32[8,8,128]{2,1,0:T(8,128)}), f32[8,8,128]{2,1,0:T(8,128)S(1)}, u32[]{:S(2)}, u32[]{:S(2)}) %all-to-all-start) | async-done | bytes 32800 | tf_op jit(solution)/shard_map/all_to_all | solution.py:227
  100.6 1.8 %collective-permute-start.19 = (bf16[4,128,1024]{2,1,0:T(8,128)(2,1)}, bf16[4,128,1024]{2,1,0:T(8,128)(2,1)}, u32[]{:S(2)}, u32[]{:S(2)}) collective-permute-start(bf16[4,128,1024]{2,1,0:T(8,128)(2,1)} %collective-permute-done.13.refs_1_), channel_id=1, source_target_pairs={{0,4},{4,0},{1,5},{5,1},{2,6},{6,2},{3,7},{7,3},{8,12},{12,8},{9,1... | collective-permute-start | bytes 3145736 | tf_op jit(solution)/shard_map/ppermute | solution.py:64
  102.4 0.1 collective-permute-start.20
  102.5 0.4 collective-permute-start.21
  103.0 0.6 broadcast_in_dim.5
  103.6 4.0 %all-to-all-start.1 = ((f32[16,8,128]{2,1,0:T(8,128)}), f32[16,8,128]{2,1,0:T(8,128)S(1)}, u32[]{:S(2)}, u32[]{:S(2)}) async-start(f32[16,8,128]{2,1,0:T(8,128)} %broadcast_in_dim.5), calls=%async_computation.1 | async-start | bytes 131072 | tf_op jit(solution)/shard_map/all_to_all | solution.py:227
  107.6 0.5 collective-permute-done.21.refs_7_
  108.1 9.0 %shard_map.83 = bf16[512,4096]{1,0:T(8,128)(2,1)} custom-call(s32[4]{0:T(128)S(1)} %pad_add_fusion.at_ref, bf16[512,1024]{1,0:T(8,128)(2,1)S(1)} %copy-done.6, bf16[4,128,1024]{2,1,0:T(8,128)(2,1)S(1)} %pad_maximum_fusion.refs_0_, bf16[4,128,1024]{2,1,0:T(8,128)(2,1)} %collective-permute-done.13.refs_1_, ...), custom_call_target="tpu_custom_call" | custom-call | flops 4294967296 | bytes 13631488 | tf_op jit(solution)/shard_map/pallas_call | solution.py:280
  117.1 0.9 shard_map.84
  (32 shorter events, 0.2 us)
Async XLA Ops:
  0.7 2.2 %copy-start = (bf16[512,4096]{1,0:T(8,128)(2,1)S(1)}, bf16[512,4096]{1,0:T(8,128)(2,1)}, u32[]{:S(2)}) copy-start(bf16[512,4096]{1,0:T(8,128)(2,1)} %hidden_ref.1) | copy-start | bytes 12582916
  2.9 5.0 %copy-start.1 = (bf16[512,1024]{1,0:T(8,128)(2,1)S(1)}, bf16[512,1024]{1,0:T(8,128)(2,1)}, u32[]{:S(2)}) copy-start(bf16[512,1024]{1,0:T(8,128)(2,1)} %cot_ref.1) | copy-start | bytes 3145732
  2.9 5.0 %copy-start.3 = (s32[2,4]{1,0:T(2,128)S(1)}, s32[2,4]{1,0:T(2,128)}, u32[]{:S(2)}) copy-start(s32[2,4]{1,0:T(2,128)} %len_ref.1) | copy-start | bytes 100
  4.6 9.5 %collective-permute-start.1 = (bf16[512,2048]{1,0:T(8,128)(2,1)S(1)}, bf16[512,2048]{1,0:T(8,128)(2,1)S(1)}, u32[]{:S(2)}, u32[]{:S(2)}) collective-permute-start(bf16[512,2048]{1,0:T(8,128)(2,1)S(1)} %get-tuple-element.41), channel_id=1, source_target_pairs={{0,4},{4,0},{1,5},{5,1},{2,6},{6,2},{3,7},{7,3},{8,12},{12,8},{9,1... | collective-permute-start | bytes 6291464 | tf_op jit(solution)/shard_map/ppermute | solution.py:64
  10.5 1.0 copy-start.5
  11.5 2.7 %collective-permute-start = (bf16[1024,512]{1,0:T(8,128)(2,1)S(1)}, bf16[1024,512]{1,0:T(8,128)(2,1)S(1)}, u32[]{:S(2)}, u32[]{:S(2)}) collective-permute-start(bf16[1024,512]{1,0:T(8,128)(2,1)S(1)} %get-tuple-element.39.own_t), channel_id=1, source_target_pairs={{0,4},{4,0},{1,5},{5,1},{2,6},{6,2},{3,7},{7,3},{8,12},{12,8},{9,1... | collective-permute-start | bytes 3145736 | tf_op jit(solution)/shard_map/ppermute | solution.py:64
  18.2 30.0 %collective-permute-start.7 = (bf16[1024,512]{1,0:T(8,128)(2,1)}, bf16[1024,512]{1,0:T(8,128)(2,1)S(1)}, u32[]{:S(2)}, u32[]{:S(2)}) collective-permute-start(bf16[1024,512]{1,0:T(8,128)(2,1)} %get-tuple-element.48), channel_id=1, source_target_pairs={{0,64},{4,20},{16,80},{20,36},{32,96},{36,52},{48,112},{52,4},{64,... | collective-permute-start | bytes 3145736 | tf_op jit(solution)/shard_map/ppermute | solution.py:50
  18.2 6.5 %copy-start.2 = (bf16[64,1024]{1,0:T(8,128)(2,1)S(1)}, bf16[64,1024]{1,0:T(8,128)(2,1)}, u32[]{:S(2)}) copy-start(bf16[64,1024]{1,0:T(8,128)(2,1)} %weight.1) | copy-start | bytes 393220
  18.3 30.0 %collective-permute-start.8 = (bf16[1024,512]{1,0:T(8,128)(2,1)}, bf16[1024,512]{1,0:T(8,128)(2,1)}, u32[]{:S(2)}, u32[]{:S(2)}) collective-permute-start(bf16[1024,512]{1,0:T(8,128)(2,1)} %get-tuple-element.49), channel_id=1, source_target_pairs={{0,128},{4,36},{16,144},{20,52},{32,160},{36,4},{48,176},{52,20},{... | collective-permute-start | bytes 3145736 | tf_op jit(solution)/shard_map/ppermute | solution.py:50
  23.8 24.5 %collective-permute-start.9 = (bf16[1024,512]{1,0:T(8,128)(2,1)}, bf16[1024,512]{1,0:T(8,128)(2,1)}, u32[]{:S(2)}, u32[]{:S(2)}) collective-permute-start(bf16[1024,512]{1,0:T(8,128)(2,1)} %get-tuple-element.50), channel_id=1, source_target_pairs={{0,192},{4,52},{16,208},{20,4},{32,224},{36,20},{48,240},{52,36},{... | collective-permute-start | bytes 3145736 | tf_op jit(solution)/shard_map/ppermute | solution.py:50
  24.8 9.6 %collective-permute-start.2 = (bf16[64,1024]{1,0:T(8,128)(2,1)S(1)}, bf16[64,1024]{1,0:T(8,128)(2,1)S(1)}, u32[]{:S(2)}, u32[]{:S(2)}) collective-permute-start(bf16[64,1024]{1,0:T(8,128)(2,1)S(1)} %copy-done.2), channel_id=1, source_target_pairs={{0,8},{4,0},{8,12},{12,4},{1,9},{5,1},{9,13},{13,5},{2,10},{6,2},{... | collective-permute-start | bytes 393224 | tf_op jit(solution)/shard_map/ppermute | solution.py:309
  25.6 12.7 %collective-permute-start.3 = (bf16[64,1024]{1,0:T(8,128)(2,1)S(1)}, bf16[64,1024]{1,0:T(8,128)(2,1)S(1)}, u32[]{:S(2)}, u32[]{:S(2)}) collective-permute-start(bf16[64,1024]{1,0:T(8,128)(2,1)S(1)} %copy-done.2), channel_id=1, source_target_pairs={{4,8},{8,4},{5,9},{9,5},{6,10},{10,6},{7,11},{11,7},{20,24},{24,20... | collective-permute-start | bytes 393224 | tf_op jit(solution)/shard_map/ppermute | solution.py:310
  38.4 9.3 %collective-permute-start.4 = (bf16[128,1024]{1,0:T(8,128)(2,1)S(1)}, bf16[128,1024]{1,0:T(8,128)(2,1)S(1)}, u32[]{:S(2)}, u32[]{:S(2)}) collective-permute-start(bf16[128,1024]{1,0:T(8,128)(2,1)S(1)} %pad_maximum_fusion.1), channel_id=1, source_target_pairs={{0,64},{4,20},{16,80},{20,36},{32,96},{36,52},{48,112},{52,4},{64,... | collective-permute-start | bytes 786440 | tf_op jit(solution)/shard_map/ppermute | solution.py:50
  39.2 9.1 %collective-permute-start.5 = (bf16[128,1024]{1,0:T(8,128)(2,1)S(1)}, bf16[128,1024]{1,0:T(8,128)(2,1)S(1)}, u32[]{:S(2)}, u32[]{:S(2)}) collective-permute-start(bf16[128,1024]{1,0:T(8,128)(2,1)S(1)} %pad_maximum_fusion.1), channel_id=1, source_target_pairs={{0,192},{4,52},{16,208},{20,4},{32,224},{36,20},{48,240},{52,36},{... | collective-permute-start | bytes 786440 | tf_op jit(solution)/shard_map/ppermute | solution.py:50
  50.5 9.6 %collective-permute-start.10 = (bf16[1024,128]{1,0:T(8,128)(2,1)S(1)}, bf16[1024,128]{1,0:T(8,128)(2,1)S(1)}, u32[]{:S(2)}, u32[]{:S(2)}) collective-permute-start(bf16[1024,128]{1,0:T(8,128)(2,1)S(1)} %get-tuple-element.52), channel_id=1, source_target_pairs={{0,16},{4,68},{16,32},{20,84},{32,48},{36,100},{48,0},{52,116},{64... | collective-permute-start | bytes 786440 | tf_op jit(solution)/shard_map/ppermute | solution.py:60
  50.6 9.5 %collective-permute-start.11 = (bf16[1024,128]{1,0:T(8,128)(2,1)S(1)}, bf16[1024,128]{1,0:T(8,128)(2,1)S(1)}, u32[]{:S(2)}, u32[]{:S(2)}) collective-permute-start(bf16[1024,128]{1,0:T(8,128)(2,1)S(1)} %get-tuple-element.53), channel_id=1, source_target_pairs={{0,32},{4,132},{16,48},{20,148},{32,0},{36,164},{48,16},{52,180},{... | collective-permute-start | bytes 786440 | tf_op jit(solution)/shard_map/ppermute | solution.py:60
  53.2 7.7 %collective-permute-start.12 = (bf16[1024,128]{1,0:T(8,128)(2,1)S(1)}, bf16[1024,128]{1,0:T(8,128)(2,1)S(1)}, u32[]{:S(2)}, u32[]{:S(2)}) collective-permute-start(bf16[1024,128]{1,0:T(8,128)(2,1)S(1)} %get-tuple-element.54), channel_id=1, source_target_pairs={{0,48},{4,196},{16,0},{20,212},{32,16},{36,228},{48,32},{52,244},{... | collective-permute-start | bytes 786440 | tf_op jit(solution)/shard_map/ppermute | solution.py:60
  54.0 9.9 %collective-permute-start.6 = (bf16[128,1024]{1,0:T(8,128)(2,1)S(1)}, bf16[128,1024]{1,0:T(8,128)(2,1)S(1)}, u32[]{:S(2)}, u32[]{:S(2)}) collective-permute-start(bf16[128,1024]{1,0:T(8,128)(2,1)S(1)} %pad_maximum_fusion.1), channel_id=1, source_target_pairs={{0,128},{4,36},{16,144},{20,52},{32,160},{36,4},{48,176},{52,20},{... | collective-permute-start | bytes 786440 | tf_op jit(solution)/shard_map/ppermute | solution.py:50
  60.9 47.2 %copy-start.6 = (bf16[512,1024]{1,0:T(8,128)(2,1)S(1)}, bf16[512,1024]{1,0:T(8,128)(2,1)}, u32[]{:S(2)}) copy-start(bf16[512,1024]{1,0:T(8,128)(2,1)} %copy-done.5) | copy-start | bytes 3145732
  64.1 36.5 %collective-permute-start.13 = (bf16[4,128,1024]{2,1,0:T(8,128)(2,1)S(1)}, bf16[4,128,1024]{2,1,0:T(8,128)(2,1)}, u32[]{:S(2)}, u32[]{:S(2)}) collective-permute-start(bf16[4,128,1024]{2,1,0:T(8,128)(2,1)S(1)} %pad_maximum_fusion.refs_0_), channel_id=1, source_target_pairs={{0,16},{4,68},{16,32},{20,84},{32,48},{36,100},{48,0},{52,116},{64... | collective-permute-start | bytes 3145736 | tf_op jit(solution)/shard_map/ppermute | solution.py:60
  64.7 35.9 %collective-permute-start.14 = (bf16[4,128,1024]{2,1,0:T(8,128)(2,1)S(1)}, bf16[4,128,1024]{2,1,0:T(8,128)(2,1)}, u32[]{:S(2)}, u32[]{:S(2)}) collective-permute-start(bf16[4,128,1024]{2,1,0:T(8,128)(2,1)S(1)} %pad_maximum_fusion.refs_0_), channel_id=1, source_target_pairs={{0,32},{4,132},{16,48},{20,148},{32,0},{36,164},{48,16},{52,180},{... | collective-permute-start | bytes 3145736 | tf_op jit(solution)/shard_map/ppermute | solution.py:60
  65.8 34.8 %collective-permute-start.15 = (bf16[4,128,1024]{2,1,0:T(8,128)(2,1)S(1)}, bf16[4,128,1024]{2,1,0:T(8,128)(2,1)}, u32[]{:S(2)}, u32[]{:S(2)}) collective-permute-start(bf16[4,128,1024]{2,1,0:T(8,128)(2,1)S(1)} %pad_maximum_fusion.refs_0_), channel_id=1, source_target_pairs={{0,48},{4,196},{16,0},{20,212},{32,16},{36,228},{48,32},{52,244},{... | collective-permute-start | bytes 3145736 | tf_op jit(solution)/shard_map/ppermute | solution.py:60
  67.8 12.1 %collective-permute-start.16 = (bf16[64,1024]{1,0:T(8,128)(2,1)S(1)}, bf16[64,1024]{1,0:T(8,128)(2,1)S(1)}, u32[]{:S(2)}, u32[]{:S(2)}) collective-permute-start(bf16[64,1024]{1,0:T(8,128)(2,1)S(1)} %get-tuple-element.55), channel_id=1, source_target_pairs={{0,4},{4,12},{8,0},{12,8},{1,5},{5,13},{9,1},{13,9},{2,6},{6,14},{... | collective-permute-start | bytes 393224 | tf_op jit(solution)/shard_map/ppermute | solution.py:324
  73.5 10.3 %collective-permute-start.17 = (bf16[64,1024]{1,0:T(8,128)(2,1)S(1)}, bf16[64,1024]{1,0:T(8,128)(2,1)S(1)}, u32[]{:S(2)}, u32[]{:S(2)}) collective-permute-start(bf16[64,1024]{1,0:T(8,128)(2,1)S(1)} %get-tuple-element.61), channel_id=1, source_target_pairs={{8,4},{4,8},{9,5},{5,9},{10,6},{6,10},{11,7},{7,11},{24,20},{20,24... | collective-permute-start | bytes 393224 | tf_op jit(solution)/shard_map/ppermute | solution.py:325
  87.0 13.6 %all-to-all-start = ((f32[8,8,128]{2,1,0:T(8,128)}), f32[8,8,128]{2,1,0:T(8,128)S(1)}, u32[]{:S(2)}, u32[]{:S(2)}) async-start(f32[8,8,128]{2,1,0:T(8,128)} %broadcast_in_dim.4), calls=%async_computation | async-start | bytes 65536 | tf_op jit(solution)/shard_map/all_to_all | solution.py:227
  93.7 13.9 %collective-permute-start.18 = (bf16[4,128,1024]{2,1,0:T(8,128)(2,1)S(1)}, bf16[4,128,1024]{2,1,0:T(8,128)(2,1)}, u32[]{:S(2)}, u32[]{:S(2)}) collective-permute-start(bf16[4,128,1024]{2,1,0:T(8,128)(2,1)S(1)} %pad_maximum_fusion.refs_0_), channel_id=1, source_target_pairs={{0,4},{4,0},{1,5},{5,1},{2,6},{6,2},{3,7},{7,3},{8,12},{12,8},{9,1... | collective-permute-start | bytes 3145736 | tf_op jit(solution)/shard_map/ppermute | solution.py:64
  100.6 7.0 %collective-permute-start.19 = (bf16[4,128,1024]{2,1,0:T(8,128)(2,1)}, bf16[4,128,1024]{2,1,0:T(8,128)(2,1)}, u32[]{:S(2)}, u32[]{:S(2)}) collective-permute-start(bf16[4,128,1024]{2,1,0:T(8,128)(2,1)} %collective-permute-done.13.refs_1_), channel_id=1, source_target_pairs={{0,4},{4,0},{1,5},{5,1},{2,6},{6,2},{3,7},{7,3},{8,12},{12,8},{9,1... | collective-permute-start | bytes 3145736 | tf_op jit(solution)/shard_map/ppermute | solution.py:64
  102.4 5.2 %collective-permute-start.20 = (bf16[4,128,1024]{2,1,0:T(8,128)(2,1)}, bf16[4,128,1024]{2,1,0:T(8,128)(2,1)}, u32[]{:S(2)}, u32[]{:S(2)}) collective-permute-start(bf16[4,128,1024]{2,1,0:T(8,128)(2,1)} %collective-permute-done.14.refs_2_), channel_id=1, source_target_pairs={{0,4},{4,0},{1,5},{5,1},{2,6},{6,2},{3,7},{7,3},{8,12},{12,8},{9,1... | collective-permute-start | bytes 3145736 | tf_op jit(solution)/shard_map/ppermute | solution.py:64
  102.5 5.5 %collective-permute-start.21 = (bf16[4,128,1024]{2,1,0:T(8,128)(2,1)}, bf16[4,128,1024]{2,1,0:T(8,128)(2,1)}, u32[]{:S(2)}, u32[]{:S(2)}) collective-permute-start(bf16[4,128,1024]{2,1,0:T(8,128)(2,1)} %collective-permute-done.15.refs_3_), channel_id=1, source_target_pairs={{0,4},{4,0},{1,5},{5,1},{2,6},{6,2},{3,7},{7,3},{8,12},{12,8},{9,1... | collective-permute-start | bytes 3145736 | tf_op jit(solution)/shard_map/ppermute | solution.py:64
  103.6 13.5 %all-to-all-start.1 = ((f32[16,8,128]{2,1,0:T(8,128)}), f32[16,8,128]{2,1,0:T(8,128)S(1)}, u32[]{:S(2)}, u32[]{:S(2)}) async-start(f32[16,8,128]{2,1,0:T(8,128)} %broadcast_in_dim.5), calls=%async_computation.1 | async-start | bytes 131072 | tf_op jit(solution)/shard_map/all_to_all | solution.py:227
  108.1 9.0 %copy-start.4 = (f32[64]{0:T(128)S(1)}, f32[64]{0:T(128)}, u32[]{:S(2)}) copy-start(f32[64]{0:T(128)} %param.7) | copy-start | bytes 772
where the time goes:
time: 118 us
  starting transfers between devices  54.3 us (46%)
  waiting for transfers between devices  30.9 us (26%)
  Pallas kernels  24.7 us (21%)
  local copies, waits for them, and re-layouts  4.43 us (4%)
  blocking collectives  2.46 us (2%)
    all_to_all x2, starting transfers between devices, send_all(): return lax.all_to_all(copies, axes, 0, 0, tiled=True)  10.7 us
    ppermute x6, waiting for transfers between devices, spread(): return lax.ppermute(value, ('x', 'y', 'c'), pairs)  9.43 us
    pallas_call x1, Pallas kernels, input_product(): call(input_kernel, [struct((512, 4096), BF)], [SM] + [VM] * 9, out_specs=...  9 us
    ppermute x1, starting transfers between devices, shards(): p_w = lax.ppermute(weight, ('zh', 'c'), [(1, 2), (2, 1)])  8.69 us
    ppermute x6, starting transfers between devices, spread(): return lax.ppermute(value, ('x', 'y', 'c'), pairs)  8.52 us
    pallas_call x2, Pallas kernels, grad_parts(): call(functools.partial(grad_kernel, steps), outs, [SM, VM, VM, VM, VM], v...  7.43 us
    ppermute x6, starting transfers between devices, spread_across(): return lax.ppermute(value, ('x', 'y', 'c'), pairs)  7.2 us
    ppermute x1, starting transfers between devices, shards(): p_in = lax.ppermute(p_out, ('zh', 'c'), [(2, 1), (1, 2)])  6.42 us
  transfers between devices with their start and end apart: 24, of which 10 were waited for; matrix products, arithmetic and copies ran while one was open for 1% of the time, Pallas kernels for 13%

commit v1 on v0

--- a/solution.py
+++ b/solution.py
@@ -64,7 +64,7 @@
     return lax.ppermute(value, "c", [(0, 1), (1, 0)])
 
 
-def rope_kernel(len_ref, cot_ref, grad_ref, turned_ref):
+def rope_kernel(len_ref, cot_ref, turned_ref):
     lane = lax.broadcasted_iota(jnp.int32, (LEN, HD), 1)
     place = lax.broadcasted_iota(jnp.int32, (LEN, HD), 0)
     index = jnp.where(lane < HD // 2, lane, lane - HD // 2).astype(F32)
@@ -90,7 +90,6 @@
             value = cot_ref[rows, cols]
             swapped = jnp.dot(value, swap, preferred_element_type=F32)
             out = (value.astype(F32) * cos + swapped * sin).astype(BF)
-            grad_ref[rows, cols] = out
             turned = lax.dot_general(
                 eye, out, (((1,), (1,)), ((), ())), preferred_element_type=F32
             )
@@ -100,11 +99,29 @@
 def rope(doc_lengths, cotangent):
     return call(
         rope_kernel,
-        [struct((512, KVW), BF), struct((KVW, 512), BF)],
+        [struct((KVW, 512), BF)],
         [SM, VM],
         vmem=12,
         moved=3 * MIB,
-    )(doc_lengths, cotangent)
+    )(doc_lengths, cotangent)[0]
+
+
+def turn_back_kernel(turned_ref, grad_ref):
+    row = lax.broadcasted_iota(jnp.int32, (256, 256), 0)
+    col = lax.broadcasted_iota(jnp.int32, (256, 256), 1)
+    eye = (row == col).astype(F32).astype(BF)
+    for seq in range(2):
+        rows = slice(seq * LEN, seq * LEN + LEN)
+        value = lax.dot_general(
+            eye, turned_ref[:, rows], (((1,), (1,)), ((), ())), preferred_element_type=F32
+        )
+        grad_ref[rows, :] = value.astype(BF)
+
+
+def turn_back(turned):
+    return call(
+        turn_back_kernel, [struct((512, KVW), BF)], [VM], vmem=12, moved=2 * MIB
+    )(turned)[0]
 
 
 def split_kernel(at_ref, hidden_ref, mine, other):
@@ -298,12 +315,15 @@
 
     mine, other_h = split(at, hidden)
     other_h = swap_cores(other_h)
-    key_grad, turned = rope(doc_lengths, key_cotangent)
+    turned = rope(doc_lengths, key_cotangent)
     other_t = swap_cores(turned)
 
     part2, part1 = grad_parts((2, 1), at, turned, other_t, mine, other_h)
     part3, part0 = grad_parts((3, 0), at, turned, other_t, mine, other_h)
     parts = [part0] + [spread(v, j) for j, v in ((1, part1), (2, part2), (3, part3))]
+
+    kept, _ = lax.optimization_barrier((turned, part0))
+    key_grad = turn_back(kept)
 
     weight, _ = lax.optimization_barrier((key_weight, part0))
     q_w = lax.ppermute(weight, ("zh", "c"), [(0, 2), (1, 0), (2, 3), (3, 1)])
@@ -315,7 +335,7 @@
     )
 
     near = [spread(rows, 1), spread(rows, 3)]
-    parts[0], rows, *near = lax.optimization_barrier((parts[0], rows, *near))
+    parts[0], rows, key_grad, *near = lax.optimization_barrier((parts[0], rows, key_grad, *near))
 
     sums = first_sum(at, parts)
     ring = [rows, near[0], spread(rows, 2), near[1]]

time: 118 us -> 118 us (level)
  waiting for transfers between devices: 30.9 us -> 29 us
    ppermute x6, waiting for transfers between devices: 9.43 us -> 8.01 us  [spread(): return lax.ppermute(value, ('x', 'y', 'c'), pairs)]
    pallas_call x1 -> x2, Pallas kernels: 2.54 us -> 2.98 us  [the longest x1 2.51 us: rope(): call(rope_kernel, [struct((KVW, 512), BF)], [SM, VM], vmem=12, moved=3 *...]
  transfers between devices with their start and end apart: 24 -> 24, of which waited for: 10 -> 10; matrix products, arithmetic and copies ran while one was open for 1% -> 1% of each run, Pallas kernels for 13% -> 14%
where the time goes in v1:
time: 118 us
  starting transfers between devices  55 us (47%)
  waiting for transfers between devices  29 us (25%)
  Pallas kernels  25.5 us (22%)
  local copies, waits for them, and re-layouts  4.43 us (4%)
  blocking collectives  2.46 us (2%)
    all_to_all x2, starting transfers between devices, send_all(): return lax.all_to_all(copies, axes, 0, 0, tiled=True)  10.7 us
    pallas_call x1, Pallas kernels, input_product(): call(input_kernel, [struct((512, 4096), BF)], [SM] + [VM] * 9, out_specs=...  8.99 us
    ppermute x1, starting transfers between devices, shards(): p_w = lax.ppermute(weight, ('zh', 'c'), [(1, 2), (2, 1)])  8.69 us
    ppermute x6, starting transfers between devices, spread(): return lax.ppermute(value, ('x', 'y', 'c'), pairs)  8.66 us
    ppermute x6, waiting for transfers between devices, spread(): return lax.ppermute(value, ('x', 'y', 'c'), pairs)  8.01 us
    pallas_call x2, Pallas kernels, grad_parts(): call(functools.partial(grad_kernel, steps), outs, [SM, VM, VM, VM, VM], v...  7.42 us
    ppermute x6, starting transfers between devices, spread_across(): return lax.ppermute(value, ('x', 'y', 'c'), pairs)  7.16 us
    ppermute x1, starting transfers between devices, shards(): p_in = lax.ppermute(p_out, ('zh', 'c'), [(2, 1), (1, 2)])  6.67 us
  transfers between devices with their start and end apart: 24, of which 10 were waited for; matrix products, arithmetic and copies ran while one was open for 1% of the time, Pallas kernels for 14%

profile of v1, /device:TPU:1, one launch (start us, length us, event | category | flops | bytes accessed | tf_op | source)
XLA Modules:
  0.0 117.5 jit_solution(16217122376204609430)
XLA Ops:
  0.7 2.2 %copy-done = bf16[512,4096]{1,0:T(8,128)(2,1)S(1)} copy-done((bf16[512,4096]{1,0:T(8,128)(2,1)S(1)}, bf16[512,4096]{1,0:T(8,128)(2,1)}, u32[]{:S(2)}) %copy-start) | copy-done | bytes 4194328
  2.9 1.7 %shard_map.77 = (bf16[512,2048]{1,0:T(8,128)(2,1)S(1)}, bf16[512,2048]{1,0:T(8,128)(2,1)S(1)}) custom-call(s32[4]{0:T(128)S(1)} %pad_add_fusion.at_ref, bf16[512,4096]{1,0:T(8,128)(2,1)S(1)} %copy-done), custom_call_target="tpu_custom_call" | custom-call | bytes 8388608 | tf_op jit(solution)/shard_map/pallas_call | solution.py:137
  4.6 3.3 %collective-permute-start.1 = (bf16[512,2048]{1,0:T(8,128)(2,1)S(1)}, bf16[512,2048]{1,0:T(8,128)(2,1)S(1)}, u32[]{:S(2)}, u32[]{:S(2)}) collective-permute-start(bf16[512,2048]{1,0:T(8,128)(2,1)S(1)} %get-tuple-element.39), channel_id=1, source_target_pairs={{0,4},{4,0},{1,5},{5,1},{2,6},{6,2},{3,7},{7,3},{8,12},{12,8},{9,1... | collective-permute-start | bytes 6291464 | tf_op jit(solution)/shard_map/ppermute | solution.py:64
  8.0 2.5 %shard_map.76.own_t.turned_ref = bf16[1024,512]{1,0:T(8,128)(2,1)S(1)} custom-call(s32[2,4]{1,0:T(2,128)S(1)} %copy-done.5, bf16[512,1024]{1,0:T(8,128)(2,1)S(1)} %copy-done.3), custom_call_target="tpu_custom_call" | custom-call | bytes 3145728 | tf_op jit(solution)/shard_map/pallas_call | solution.py:100
  10.5 0.1 collective-permute-start
  10.6 2.6 %collective-permute-done.other_t = bf16[1024,512]{1,0:T(8,128)(2,1)S(1)} collective-permute-done((bf16[1024,512]{1,0:T(8,128)(2,1)S(1)}, bf16[1024,512]{1,0:T(8,128)(2,1)S(1)}, u32[]{:S(2)}, u32[]{:S(2)}) %collective-permute-start) | collective-permute-done | bytes 1048608 | tf_op jit(solution)/shard_map/ppermute | solution.py:64
  13.2 4.1 %shard_map.80 = (bf16[1024,512]{1,0:T(8,128)(2,1)}, bf16[1024,512]{1,0:T(8,128)(2,1)}) custom-call(s32[4]{0:T(128)S(1)} %pad_add_fusion.at_ref, bf16[1024,512]{1,0:T(8,128)(2,1)S(1)} %shard_map.76.own_t.turned_ref, bf16[1024,512]{1,0:T(8,128)(2,1)S(1)} %collective-permute-done.other_t, bf16[512,2048]{1,0:T(8,128)(2,1)S(1)} %get-tuple-element.38.mine, ...), custom_call_target="tpu_custom_call" | custom-call | flops 2147483648 | bytes 8388608 | tf_op jit(solution)/shard_map/pallas_call | solution.py:173
  17.4 2.2 %collective-permute-start.8 = (bf16[1024,512]{1,0:T(8,128)(2,1)}, bf16[1024,512]{1,0:T(8,128)(2,1)}, u32[]{:S(2)}, u32[]{:S(2)}) collective-permute-start(bf16[1024,512]{1,0:T(8,128)(2,1)} %get-tuple-element.49), channel_id=1, source_target_pairs={{0,128},{4,36},{16,144},{20,52},{32,160},{36,4},{48,176},{52,20},{... | collective-permute-start | bytes 3145736 | tf_op jit(solution)/shard_map/ppermute | solution.py:50
  19.5 3.3 %shard_map.78 = (bf16[1024,512]{1,0:T(8,128)(2,1)}, f32[1024,512]{1,0:T(8,128)S(1)}) custom-call(s32[4]{0:T(128)S(1)} %pad_add_fusion.at_ref, bf16[1024,512]{1,0:T(8,128)(2,1)S(1)} %shard_map.76.own_t.turned_ref, bf16[1024,512]{1,0:T(8,128)(2,1)S(1)} %collective-permute-done.other_t, bf16[512,2048]{1,0:T(8,128)(2,1)S(1)} %get-tuple-element.38.mine, ...), custom_call_target="tpu_custom_call" | custom-call | flops 2147483648 | bytes 8388608 | tf_op jit(solution)/shard_map/pallas_call | solution.py:173
  22.8 1.1 collective-permute-start.9
  24.0 1.0 collective-permute-start.2
  25.0 8.7 %collective-permute-start.3 = (bf16[64,1024]{1,0:T(8,128)(2,1)S(1)}, bf16[64,1024]{1,0:T(8,128)(2,1)S(1)}, u32[]{:S(2)}, u32[]{:S(2)}) collective-permute-start(bf16[64,1024]{1,0:T(8,128)(2,1)S(1)} %copy-done.4), channel_id=1, source_target_pairs={{4,8},{8,4},{5,9},{9,5},{6,10},{10,6},{7,11},{11,7},{20,24},{24,20... | collective-permute-start | bytes 393224 | tf_op jit(solution)/shard_map/ppermute | solution.py:330
  33.7 3.8 %collective-permute-done.3 = bf16[64,1024]{1,0:T(8,128)(2,1)S(1)} collective-permute-done((bf16[64,1024]{1,0:T(8,128)(2,1)S(1)}, bf16[64,1024]{1,0:T(8,128)(2,1)S(1)}, u32[]{:S(2)}, u32[]{:S(2)}) %collective-permute-start.3) | collective-permute-done | bytes 131104 | tf_op jit(solution)/shard_map/ppermute | solution.py:330
  37.6 1.0 collective-permute-start.4
  38.5 1.8 %collective-permute-start.5 = (bf16[128,1024]{1,0:T(8,128)(2,1)S(1)}, bf16[128,1024]{1,0:T(8,128)(2,1)S(1)}, u32[]{:S(2)}, u32[]{:S(2)}) collective-permute-start(bf16[128,1024]{1,0:T(8,128)(2,1)S(1)} %pad_maximum_fusion.1), channel_id=1, source_target_pairs={{0,192},{4,52},{16,208},{20,4},{32,224},{36,20},{48,240},{52,36},{... | collective-permute-start | bytes 786440 | tf_op jit(solution)/shard_map/ppermute | solution.py:50
  40.3 0.5 shard_map.79.grad_ref
  40.8 1.0 copy-done.1
  41.8 5.0 %collective-permute-done.4 = bf16[128,1024]{1,0:T(8,128)(2,1)S(1)} collective-permute-done((bf16[128,1024]{1,0:T(8,128)(2,1)S(1)}, bf16[128,1024]{1,0:T(8,128)(2,1)S(1)}, u32[]{:S(2)}, u32[]{:S(2)}) %collective-permute-start.4) | collective-permute-done | bytes 262176 | tf_op jit(solution)/shard_map/ppermute | solution.py:50
  46.8 0.6 collective-permute-done.5
  47.4 2.6 %shard_map.81 = (f32[1024,128]{1,0:T(8,128)S(1)}, bf16[1024,128]{1,0:T(8,128)(2,1)S(1)}, bf16[1024,128]{1,0:T(8,128)(2,1)S(1)}, bf16[1024,128]{1,0:T(8,128)(2,1)S(1)}) custom-call(s32[4]{0:T(128)S(1)} %pad_add_fusion.at_ref, f32[1024,512]{1,0:T(8,128)S(1)} %get-tuple-element.47.refs_0_, bf16[1024,512]{1,0:T(8,128)(2,1)} %collective-permute-done.7.refs_1_, ...), custom_call_target="tpu_custom_call" | custom-call | bytes 6291456 | tf_op jit(solution)/shard_map/pallas_call | solution.py:195
  50.1 2.5 %collective-permute-start.11 = (bf16[1024,128]{1,0:T(8,128)(2,1)S(1)}, bf16[1024,128]{1,0:T(8,128)(2,1)S(1)}, u32[]{:S(2)}, u32[]{:S(2)}) collective-permute-start(bf16[1024,128]{1,0:T(8,128)(2,1)S(1)} %get-tuple-element.53), channel_id=1, source_target_pairs={{0,32},{4,132},{16,48},{20,148},{32,0},{36,164},{48,16},{52,180},{... | collective-permute-start | bytes 786440 | tf_op jit(solution)/shard_map/ppermute | solution.py:60
  52.6 0.9 collective-permute-start.12
  53.4 2.6 %collective-permute-start.6 = (bf16[128,1024]{1,0:T(8,128)(2,1)S(1)}, bf16[128,1024]{1,0:T(8,128)(2,1)S(1)}, u32[]{:S(2)}, u32[]{:S(2)}) collective-permute-start(bf16[128,1024]{1,0:T(8,128)(2,1)S(1)} %pad_maximum_fusion.1), channel_id=1, source_target_pairs={{0,128},{4,36},{16,144},{20,52},{32,160},{36,4},{48,176},{52,20},{... | collective-permute-start | bytes 786440 | tf_op jit(solution)/shard_map/ppermute | solution.py:50
  56.1 3.5 %collective-permute-done.10.refs_1_ = bf16[1024,128]{1,0:T(8,128)(2,1)S(1)} collective-permute-done((bf16[1024,128]{1,0:T(8,128)(2,1)S(1)}, bf16[1024,128]{1,0:T(8,128)(2,1)S(1)}, u32[]{:S(2)}, u32[]{:S(2)}) %collective-permute-start.10) | collective-permute-done | bytes 262176 | tf_op jit(solution)/shard_map/ppermute | solution.py:60
  59.6 0.6 collective-permute-done.12.refs_3_
  60.2 0.8 shard_map.82
  61.0 2.4 %collective-permute-done.6 = bf16[128,1024]{1,0:T(8,128)(2,1)S(1)} collective-permute-done((bf16[128,1024]{1,0:T(8,128)(2,1)S(1)}, bf16[128,1024]{1,0:T(8,128)(2,1)S(1)}, u32[]{:S(2)}, u32[]{:S(2)}) %collective-permute-start.6) | collective-permute-done | bytes 262176 | tf_op jit(solution)/shard_map/ppermute | solution.py:50
  63.4 0.1 pad_maximum_fusion.refs_0_
  63.5 0.5 collective-permute-start.13
  64.0 1.2 %collective-permute-start.14 = (bf16[4,128,1024]{2,1,0:T(8,128)(2,1)S(1)}, bf16[4,128,1024]{2,1,0:T(8,128)(2,1)}, u32[]{:S(2)}, u32[]{:S(2)}) collective-permute-start(bf16[4,128,1024]{2,1,0:T(8,128)(2,1)S(1)} %pad_maximum_fusion.refs_0_), channel_id=1, source_target_pairs={{0,32},{4,132},{16,48},{20,148},{32,0},{36,164},{48,16},{52,180},{... | collective-permute-start | bytes 3145736 | tf_op jit(solution)/shard_map/ppermute | solution.py:60
  65.2 2.0 %collective-permute-start.15 = (bf16[4,128,1024]{2,1,0:T(8,128)(2,1)S(1)}, bf16[4,128,1024]{2,1,0:T(8,128)(2,1)}, u32[]{:S(2)}, u32[]{:S(2)}) collective-permute-start(bf16[4,128,1024]{2,1,0:T(8,128)(2,1)S(1)} %pad_maximum_fusion.refs_0_), channel_id=1, source_target_pairs={{0,48},{4,196},{16,0},{20,212},{32,16},{36,228},{48,32},{52,244},{... | collective-permute-start | bytes 3145736 | tf_op jit(solution)/shard_map/ppermute | solution.py:60
  67.2 5.7 %collective-permute-start.16 = (bf16[64,1024]{1,0:T(8,128)(2,1)S(1)}, bf16[64,1024]{1,0:T(8,128)(2,1)S(1)}, u32[]{:S(2)}, u32[]{:S(2)}) collective-permute-start(bf16[64,1024]{1,0:T(8,128)(2,1)S(1)} %get-tuple-element.55), channel_id=1, source_target_pairs={{0,4},{4,12},{8,0},{12,8},{1,5},{5,13},{9,1},{13,9},{2,6},{6,14},{... | collective-permute-start | bytes 393224 | tf_op jit(solution)/shard_map/ppermute | solution.py:344
  72.9 6.7 %collective-permute-start.17 = (bf16[64,1024]{1,0:T(8,128)(2,1)S(1)}, bf16[64,1024]{1,0:T(8,128)(2,1)S(1)}, u32[]{:S(2)}, u32[]{:S(2)}) collective-permute-start(bf16[64,1024]{1,0:T(8,128)(2,1)S(1)} %get-tuple-element.61), channel_id=1, source_target_pairs={{8,4},{4,8},{9,5},{5,9},{10,6},{6,10},{11,7},{7,11},{24,20},{20,24... | collective-permute-start | bytes 393224 | tf_op jit(solution)/shard_map/ppermute | solution.py:345
  79.6 3.6 %collective-permute-done.17.p_in = bf16[64,1024]{1,0:T(8,128)(2,1)S(1)} collective-permute-done((bf16[64,1024]{1,0:T(8,128)(2,1)S(1)}, bf16[64,1024]{1,0:T(8,128)(2,1)S(1)}, u32[]{:S(2)}, u32[]{:S(2)}) %collective-permute-start.17) | collective-permute-done | bytes 131104 | tf_op jit(solution)/shard_map/ppermute | solution.py:345
  83.2 0.1 shard_map.83
  83.3 2.5 %psum.7 = f32[8,128]{1,0:T(8,128)S(1)} all-reduce(f32[8,128]{1,0:T(8,128)S(1)} %get-tuple-element.62), channel_id=1, replica_groups=mesh['x'=4,'y'=4,'zh'=2,'c'=2,'mp'=4] {'c'}, use_global_device_ids=true, to_apply=%region_0.1 | all-reduce | flops 1024 | bytes 8192 | tf_op jit(solution)/shard_map/psum | solution.py:353
  85.8 0.6 broadcast_in_dim.4
  86.4 6.8 %all-to-all-start = ((f32[8,8,128]{2,1,0:T(8,128)}), f32[8,8,128]{2,1,0:T(8,128)S(1)}, u32[]{:S(2)}, u32[]{:S(2)}) async-start(f32[8,8,128]{2,1,0:T(8,128)} %broadcast_in_dim.4), calls=%async_computation | async-start | bytes 65536 | tf_op jit(solution)/shard_map/all_to_all | solution.py:244
  93.2 0.6 collective-permute-start.18
  93.8 6.3 %all-to-all-done = f32[8,8,128]{2,1,0:T(8,128)S(1)} async-done(((f32[8,8,128]{2,1,0:T(8,128)}), f32[8,8,128]{2,1,0:T(8,128)S(1)}, u32[]{:S(2)}, u32[]{:S(2)}) %all-to-all-start) | async-done | bytes 32800 | tf_op jit(solution)/shard_map/all_to_all | solution.py:244
  100.1 1.8 %collective-permute-start.19 = (bf16[4,128,1024]{2,1,0:T(8,128)(2,1)}, bf16[4,128,1024]{2,1,0:T(8,128)(2,1)}, u32[]{:S(2)}, u32[]{:S(2)}) collective-permute-start(bf16[4,128,1024]{2,1,0:T(8,128)(2,1)} %collective-permute-done.13.refs_1_), channel_id=1, source_target_pairs={{0,4},{4,0},{1,5},{5,1},{2,6},{6,2},{3,7},{7,3},{8,12},{12,8},{9,1... | collective-permute-start | bytes 3145736 | tf_op jit(solution)/shard_map/ppermute | solution.py:64
  102.0 0.1 collective-permute-start.20
  102.1 0.4 collective-permute-start.21
  102.5 0.6 broadcast_in_dim.5
  103.1 3.9 %all-to-all-start.1 = ((f32[16,8,128]{2,1,0:T(8,128)}), f32[16,8,128]{2,1,0:T(8,128)S(1)}, u32[]{:S(2)}, u32[]{:S(2)}) async-start(f32[16,8,128]{2,1,0:T(8,128)} %broadcast_in_dim.5), calls=%async_computation.1 | async-start | bytes 131072 | tf_op jit(solution)/shard_map/all_to_all | solution.py:244
  107.1 0.5 collective-permute-done.21.refs_7_
  107.6 9.0 %shard_map.84 = bf16[512,4096]{1,0:T(8,128)(2,1)} custom-call(s32[4]{0:T(128)S(1)} %pad_add_fusion.at_ref, bf16[512,1024]{1,0:T(8,128)(2,1)S(1)} %copy-done.2, bf16[4,128,1024]{2,1,0:T(8,128)(2,1)S(1)} %pad_maximum_fusion.refs_0_, bf16[4,128,1024]{2,1,0:T(8,128)(2,1)} %collective-permute-done.13.refs_1_, ...), custom_call_target="tpu_custom_call" | custom-call | flops 4294967296 | bytes 13631488 | tf_op jit(solution)/shard_map/pallas_call | solution.py:297
  116.6 0.9 shard_map.85
  (33 shorter events, 0.3 us)
Async XLA Ops:
  0.7 2.2 %copy-start = (bf16[512,4096]{1,0:T(8,128)(2,1)S(1)}, bf16[512,4096]{1,0:T(8,128)(2,1)}, u32[]{:S(2)}) copy-start(bf16[512,4096]{1,0:T(8,128)(2,1)} %hidden_ref.1) | copy-start | bytes 12582916
  2.9 5.0 %copy-start.3 = (bf16[512,1024]{1,0:T(8,128)(2,1)S(1)}, bf16[512,1024]{1,0:T(8,128)(2,1)}, u32[]{:S(2)}) copy-start(bf16[512,1024]{1,0:T(8,128)(2,1)} %cot_ref.1) | copy-start | bytes 3145732
  2.9 5.0 %copy-start.5 = (s32[2,4]{1,0:T(2,128)S(1)}, s32[2,4]{1,0:T(2,128)}, u32[]{:S(2)}) copy-start(s32[2,4]{1,0:T(2,128)} %len_ref.1) | copy-start | bytes 100
  4.6 8.6 %collective-permute-start.1 = (bf16[512,2048]{1,0:T(8,128)(2,1)S(1)}, bf16[512,2048]{1,0:T(8,128)(2,1)S(1)}, u32[]{:S(2)}, u32[]{:S(2)}) collective-permute-start(bf16[512,2048]{1,0:T(8,128)(2,1)S(1)} %get-tuple-element.39), channel_id=1, source_target_pairs={{0,4},{4,0},{1,5},{5,1},{2,6},{6,2},{3,7},{7,3},{8,12},{12,8},{9,1... | collective-permute-start | bytes 6291464 | tf_op jit(solution)/shard_map/ppermute | solution.py:64
  10.5 2.8 %collective-permute-start = (bf16[1024,512]{1,0:T(8,128)(2,1)S(1)}, bf16[1024,512]{1,0:T(8,128)(2,1)S(1)}, u32[]{:S(2)}, u32[]{:S(2)}) collective-permute-start(bf16[1024,512]{1,0:T(8,128)(2,1)S(1)} %shard_map.76.own_t.turned_ref), channel_id=1, source_target_pairs={{0,4},{4,0},{1,5},{5,1},{2,6},{6,2},{3,7},{7,3},{8,12},{12,8},{9,1... | collective-permute-start | bytes 3145736 | tf_op jit(solution)/shard_map/ppermute | solution.py:64
  17.4 30.0 %collective-permute-start.7 = (bf16[1024,512]{1,0:T(8,128)(2,1)}, bf16[1024,512]{1,0:T(8,128)(2,1)}, u32[]{:S(2)}, u32[]{:S(2)}) collective-permute-start(bf16[1024,512]{1,0:T(8,128)(2,1)} %get-tuple-element.48), channel_id=1, source_target_pairs={{0,64},{4,20},{16,80},{20,36},{32,96},{36,52},{48,112},{52,4},{64,... | collective-permute-start | bytes 3145736 | tf_op jit(solution)/shard_map/ppermute | solution.py:50
  17.4 6.6 %copy-start.4 = (bf16[64,1024]{1,0:T(8,128)(2,1)S(1)}, bf16[64,1024]{1,0:T(8,128)(2,1)}, u32[]{:S(2)}) copy-start(bf16[64,1024]{1,0:T(8,128)(2,1)} %weight.1) | copy-start | bytes 393220
  17.4 30.0 %collective-permute-start.8 = (bf16[1024,512]{1,0:T(8,128)(2,1)}, bf16[1024,512]{1,0:T(8,128)(2,1)}, u32[]{:S(2)}, u32[]{:S(2)}) collective-permute-start(bf16[1024,512]{1,0:T(8,128)(2,1)} %get-tuple-element.49), channel_id=1, source_target_pairs={{0,128},{4,36},{16,144},{20,52},{32,160},{36,4},{48,176},{52,20},{... | collective-permute-start | bytes 3145736 | tf_op jit(solution)/shard_map/ppermute | solution.py:50
  22.8 24.6 %collective-permute-start.9 = (bf16[1024,512]{1,0:T(8,128)(2,1)}, bf16[1024,512]{1,0:T(8,128)(2,1)}, u32[]{:S(2)}, u32[]{:S(2)}) collective-permute-start(bf16[1024,512]{1,0:T(8,128)(2,1)} %get-tuple-element.50), channel_id=1, source_target_pairs={{0,192},{4,52},{16,208},{20,4},{32,224},{36,20},{48,240},{52,36},{... | collective-permute-start | bytes 3145736 | tf_op jit(solution)/shard_map/ppermute | solution.py:50
  24.0 9.7 %collective-permute-start.2 = (bf16[64,1024]{1,0:T(8,128)(2,1)S(1)}, bf16[64,1024]{1,0:T(8,128)(2,1)S(1)}, u32[]{:S(2)}, u32[]{:S(2)}) collective-permute-start(bf16[64,1024]{1,0:T(8,128)(2,1)S(1)} %copy-done.4), channel_id=1, source_target_pairs={{0,8},{4,0},{8,12},{12,4},{1,9},{5,1},{9,13},{13,5},{2,10},{6,2},{... | collective-permute-start | bytes 393224 | tf_op jit(solution)/shard_map/ppermute | solution.py:329
  25.0 12.5 %collective-permute-start.3 = (bf16[64,1024]{1,0:T(8,128)(2,1)S(1)}, bf16[64,1024]{1,0:T(8,128)(2,1)S(1)}, u32[]{:S(2)}, u32[]{:S(2)}) collective-permute-start(bf16[64,1024]{1,0:T(8,128)(2,1)S(1)} %copy-done.4), channel_id=1, source_target_pairs={{4,8},{8,4},{5,9},{9,5},{6,10},{10,6},{7,11},{11,7},{20,24},{24,20... | collective-permute-start | bytes 393224 | tf_op jit(solution)/shard_map/ppermute | solution.py:330
  37.6 9.2 %collective-permute-start.4 = (bf16[128,1024]{1,0:T(8,128)(2,1)S(1)}, bf16[128,1024]{1,0:T(8,128)(2,1)S(1)}, u32[]{:S(2)}, u32[]{:S(2)}) collective-permute-start(bf16[128,1024]{1,0:T(8,128)(2,1)S(1)} %pad_maximum_fusion.1), channel_id=1, source_target_pairs={{0,64},{4,20},{16,80},{20,36},{32,96},{36,52},{48,112},{52,4},{64,... | collective-permute-start | bytes 786440 | tf_op jit(solution)/shard_map/ppermute | solution.py:50
  38.5 8.9 %collective-permute-start.5 = (bf16[128,1024]{1,0:T(8,128)(2,1)S(1)}, bf16[128,1024]{1,0:T(8,128)(2,1)S(1)}, u32[]{:S(2)}, u32[]{:S(2)}) collective-permute-start(bf16[128,1024]{1,0:T(8,128)(2,1)S(1)} %pad_maximum_fusion.1), channel_id=1, source_target_pairs={{0,192},{4,52},{16,208},{20,4},{32,224},{36,20},{48,240},{52,36},{... | collective-permute-start | bytes 786440 | tf_op jit(solution)/shard_map/ppermute | solution.py:50
  40.8 1.0 copy-start.1
  50.0 9.6 %collective-permute-start.10 = (bf16[1024,128]{1,0:T(8,128)(2,1)S(1)}, bf16[1024,128]{1,0:T(8,128)(2,1)S(1)}, u32[]{:S(2)}, u32[]{:S(2)}) collective-permute-start(bf16[1024,128]{1,0:T(8,128)(2,1)S(1)} %get-tuple-element.52), channel_id=1, source_target_pairs={{0,16},{4,68},{16,32},{20,84},{32,48},{36,100},{48,0},{52,116},{64... | collective-permute-start | bytes 786440 | tf_op jit(solution)/shard_map/ppermute | solution.py:60
  50.1 9.5 %collective-permute-start.11 = (bf16[1024,128]{1,0:T(8,128)(2,1)S(1)}, bf16[1024,128]{1,0:T(8,128)(2,1)S(1)}, u32[]{:S(2)}, u32[]{:S(2)}) collective-permute-start(bf16[1024,128]{1,0:T(8,128)(2,1)S(1)} %get-tuple-element.53), channel_id=1, source_target_pairs={{0,32},{4,132},{16,48},{20,148},{32,0},{36,164},{48,16},{52,180},{... | collective-permute-start | bytes 786440 | tf_op jit(solution)/shard_map/ppermute | solution.py:60
  52.6 7.6 %collective-permute-start.12 = (bf16[1024,128]{1,0:T(8,128)(2,1)S(1)}, bf16[1024,128]{1,0:T(8,128)(2,1)S(1)}, u32[]{:S(2)}, u32[]{:S(2)}) collective-permute-start(bf16[1024,128]{1,0:T(8,128)(2,1)S(1)} %get-tuple-element.54), channel_id=1, source_target_pairs={{0,48},{4,196},{16,0},{20,212},{32,16},{36,228},{48,32},{52,244},{... | collective-permute-start | bytes 786440 | tf_op jit(solution)/shard_map/ppermute | solution.py:60
  53.4 9.9 %collective-permute-start.6 = (bf16[128,1024]{1,0:T(8,128)(2,1)S(1)}, bf16[128,1024]{1,0:T(8,128)(2,1)S(1)}, u32[]{:S(2)}, u32[]{:S(2)}) collective-permute-start(bf16[128,1024]{1,0:T(8,128)(2,1)S(1)} %pad_maximum_fusion.1), channel_id=1, source_target_pairs={{0,128},{4,36},{16,144},{20,52},{32,160},{36,4},{48,176},{52,20},{... | collective-permute-start | bytes 786440 | tf_op jit(solution)/shard_map/ppermute | solution.py:50
  60.2 47.4 %copy-start.2 = (bf16[512,1024]{1,0:T(8,128)(2,1)S(1)}, bf16[512,1024]{1,0:T(8,128)(2,1)}, u32[]{:S(2)}) copy-start(bf16[512,1024]{1,0:T(8,128)(2,1)} %copy-done.1) | copy-start | bytes 3145732
  63.5 36.6 %collective-permute-start.13 = (bf16[4,128,1024]{2,1,0:T(8,128)(2,1)S(1)}, bf16[4,128,1024]{2,1,0:T(8,128)(2,1)}, u32[]{:S(2)}, u32[]{:S(2)}) collective-permute-start(bf16[4,128,1024]{2,1,0:T(8,128)(2,1)S(1)} %pad_maximum_fusion.refs_0_), channel_id=1, source_target_pairs={{0,16},{4,68},{16,32},{20,84},{32,48},{36,100},{48,0},{52,116},{64... | collective-permute-start | bytes 3145736 | tf_op jit(solution)/shard_map/ppermute | solution.py:60
  64.0 36.1 %collective-permute-start.14 = (bf16[4,128,1024]{2,1,0:T(8,128)(2,1)S(1)}, bf16[4,128,1024]{2,1,0:T(8,128)(2,1)}, u32[]{:S(2)}, u32[]{:S(2)}) collective-permute-start(bf16[4,128,1024]{2,1,0:T(8,128)(2,1)S(1)} %pad_maximum_fusion.refs_0_), channel_id=1, source_target_pairs={{0,32},{4,132},{16,48},{20,148},{32,0},{36,164},{48,16},{52,180},{... | collective-permute-start | bytes 3145736 | tf_op jit(solution)/shard_map/ppermute | solution.py:60
  65.2 34.9 %collective-permute-start.15 = (bf16[4,128,1024]{2,1,0:T(8,128)(2,1)S(1)}, bf16[4,128,1024]{2,1,0:T(8,128)(2,1)}, u32[]{:S(2)}, u32[]{:S(2)}) collective-permute-start(bf16[4,128,1024]{2,1,0:T(8,128)(2,1)S(1)} %pad_maximum_fusion.refs_0_), channel_id=1, source_target_pairs={{0,48},{4,196},{16,0},{20,212},{32,16},{36,228},{48,32},{52,244},{... | collective-permute-start | bytes 3145736 | tf_op jit(solution)/shard_map/ppermute | solution.py:60
  67.2 12.4 %collective-permute-start.16 = (bf16[64,1024]{1,0:T(8,128)(2,1)S(1)}, bf16[64,1024]{1,0:T(8,128)(2,1)S(1)}, u32[]{:S(2)}, u32[]{:S(2)}) collective-permute-start(bf16[64,1024]{1,0:T(8,128)(2,1)S(1)} %get-tuple-element.55), channel_id=1, source_target_pairs={{0,4},{4,12},{8,0},{12,8},{1,5},{5,13},{9,1},{13,9},{2,6},{6,14},{... | collective-permute-start | bytes 393224 | tf_op jit(solution)/shard_map/ppermute | solution.py:344
  72.9 10.3 %collective-permute-start.17 = (bf16[64,1024]{1,0:T(8,128)(2,1)S(1)}, bf16[64,1024]{1,0:T(8,128)(2,1)S(1)}, u32[]{:S(2)}, u32[]{:S(2)}) collective-permute-start(bf16[64,1024]{1,0:T(8,128)(2,1)S(1)} %get-tuple-element.61), channel_id=1, source_target_pairs={{8,4},{4,8},{9,5},{5,9},{10,6},{6,10},{11,7},{7,11},{24,20},{20,24... | collective-permute-start | bytes 393224 | tf_op jit(solution)/shard_map/ppermute | solution.py:345
  86.4 13.7 %all-to-all-start = ((f32[8,8,128]{2,1,0:T(8,128)}), f32[8,8,128]{2,1,0:T(8,128)S(1)}, u32[]{:S(2)}, u32[]{:S(2)}) async-start(f32[8,8,128]{2,1,0:T(8,128)} %broadcast_in_dim.4), calls=%async_computation | async-start | bytes 65536 | tf_op jit(solution)/shard_map/all_to_all | solution.py:244
  93.2 13.9 %collective-permute-start.18 = (bf16[4,128,1024]{2,1,0:T(8,128)(2,1)S(1)}, bf16[4,128,1024]{2,1,0:T(8,128)(2,1)}, u32[]{:S(2)}, u32[]{:S(2)}) collective-permute-start(bf16[4,128,1024]{2,1,0:T(8,128)(2,1)S(1)} %pad_maximum_fusion.refs_0_), channel_id=1, source_target_pairs={{0,4},{4,0},{1,5},{5,1},{2,6},{6,2},{3,7},{7,3},{8,12},{12,8},{9,1... | collective-permute-start | bytes 3145736 | tf_op jit(solution)/shard_map/ppermute | solution.py:64
  100.1 6.9 %collective-permute-start.19 = (bf16[4,128,1024]{2,1,0:T(8,128)(2,1)}, bf16[4,128,1024]{2,1,0:T(8,128)(2,1)}, u32[]{:S(2)}, u32[]{:S(2)}) collective-permute-start(bf16[4,128,1024]{2,1,0:T(8,128)(2,1)} %collective-permute-done.13.refs_1_), channel_id=1, source_target_pairs={{0,4},{4,0},{1,5},{5,1},{2,6},{6,2},{3,7},{7,3},{8,12},{12,8},{9,1... | collective-permute-start | bytes 3145736 | tf_op jit(solution)/shard_map/ppermute | solution.py:64
  102.0 5.1 %collective-permute-start.20 = (bf16[4,128,1024]{2,1,0:T(8,128)(2,1)}, bf16[4,128,1024]{2,1,0:T(8,128)(2,1)}, u32[]{:S(2)}, u32[]{:S(2)}) collective-permute-start(bf16[4,128,1024]{2,1,0:T(8,128)(2,1)} %collective-permute-done.14.refs_2_), channel_id=1, source_target_pairs={{0,4},{4,0},{1,5},{5,1},{2,6},{6,2},{3,7},{7,3},{8,12},{12,8},{9,1... | collective-permute-start | bytes 3145736 | tf_op jit(solution)/shard_map/ppermute | solution.py:64
  102.1 5.5 %collective-permute-start.21 = (bf16[4,128,1024]{2,1,0:T(8,128)(2,1)}, bf16[4,128,1024]{2,1,0:T(8,128)(2,1)}, u32[]{:S(2)}, u32[]{:S(2)}) collective-permute-start(bf16[4,128,1024]{2,1,0:T(8,128)(2,1)} %collective-permute-done.15.refs_3_), channel_id=1, source_target_pairs={{0,4},{4,0},{1,5},{5,1},{2,6},{6,2},{3,7},{7,3},{8,12},{12,8},{9,1... | collective-permute-start | bytes 3145736 | tf_op jit(solution)/shard_map/ppermute | solution.py:64
  103.1 13.5 %all-to-all-start.1 = ((f32[16,8,128]{2,1,0:T(8,128)}), f32[16,8,128]{2,1,0:T(8,128)S(1)}, u32[]{:S(2)}, u32[]{:S(2)}) async-start(f32[16,8,128]{2,1,0:T(8,128)} %broadcast_in_dim.5), calls=%async_computation.1 | async-start | bytes 131072 | tf_op jit(solution)/shard_map/all_to_all | solution.py:244
  107.0 9.6 %copy-start.6 = (f32[64]{0:T(128)S(1)}, f32[64]{0:T(128)}, u32[]{:S(2)}) copy-start(f32[64]{0:T(128)} %param.7) | copy-start | bytes 772

commit v2 on v1

--- a/solution.py
+++ b/solution.py
@@ -81,9 +81,10 @@
             start = start + len_ref[seq, doc - 1]
             first = jnp.where(place >= start, start, first)
         angle = (place - first).astype(F32) * frequency
-        cos = jnp.cos(angle)
-        sin = jnp.sin(angle)
-        sin = jnp.where(lane < HD // 2, sin, -sin)
+        both = jnp.cos(jnp.where(lane < HD // 2, angle, angle - 1.5707963267948966))
+        turned_over = pltpu.roll(both, HD // 2, 1)
+        cos = jnp.where(lane < HD // 2, both, turned_over)
+        sin = jnp.where(lane < HD // 2, turned_over, -both)
         rows = pl.ds(seq * LEN, LEN)
         for head in range(KVW // HD):
             cols = pl.ds(head * HD, HD)

time: 118 us -> 118 us (level)
  no operation moved by 1% of the time
where the time goes in v2:
time: 118 us
  starting transfers between devices  55 us (47%)
  waiting for transfers between devices  29.1 us (25%)
  Pallas kernels  25.3 us (21%)
  local copies, waits for them, and re-layouts  4.43 us (4%)
  blocking collectives  2.46 us (2%)
    all_to_all x2, starting transfers between devices, send_all(): return lax.all_to_all(copies, axes, 0, 0, tiled=True)  10.7 us
    pallas_call x1, Pallas kernels, input_product(): call(input_kernel, [struct((512, 4096), BF)], [SM] + [VM] * 9, out_specs=...  8.99 us
    ppermute x1, starting transfers between devices, shards(): p_w = lax.ppermute(weight, ('zh', 'c'), [(1, 2), (2, 1)])  8.69 us
    ppermute x6, starting transfers between devices, spread(): return lax.ppermute(value, ('x', 'y', 'c'), pairs)  8.66 us
    ppermute x6, waiting for transfers between devices, spread(): return lax.ppermute(value, ('x', 'y', 'c'), pairs)  8.01 us
    pallas_call x2, Pallas kernels, grad_parts(): call(functools.partial(grad_kernel, steps), outs, [SM, VM, VM, VM, VM], v...  7.42 us
    ppermute x6, starting transfers between devices, spread_across(): return lax.ppermute(value, ('x', 'y', 'c'), pairs)  7.16 us
    ppermute x1, starting transfers between devices, shards(): p_in = lax.ppermute(p_out, ('zh', 'c'), [(2, 1), (1, 2)])  6.67 us
  transfers between devices with their start and end apart: 24, of which 10 were waited for; matrix products, arithmetic and copies ran while one was open for 1% of the time, Pallas kernels for 14%

profile of v2, /device:TPU:1, one launch (start us, length us, event | category | flops | bytes accessed | tf_op | source)
XLA Modules:
  0.0 117.5 jit_solution(13144652880377036841)
XLA Ops:
  0.7 2.2 %copy-done = bf16[512,4096]{1,0:T(8,128)(2,1)S(1)} copy-done((bf16[512,4096]{1,0:T(8,128)(2,1)S(1)}, bf16[512,4096]{1,0:T(8,128)(2,1)}, u32[]{:S(2)}) %copy-start) | copy-done | bytes 4194328
  2.9 1.7 %shard_map.77 = (bf16[512,2048]{1,0:T(8,128)(2,1)S(1)}, bf16[512,2048]{1,0:T(8,128)(2,1)S(1)}) custom-call(s32[4]{0:T(128)S(1)} %pad_add_fusion.at_ref, bf16[512,4096]{1,0:T(8,128)(2,1)S(1)} %copy-done), custom_call_target="tpu_custom_call" | custom-call | bytes 8388608 | tf_op jit(solution)/shard_map/pallas_call | solution.py:138
  4.6 3.3 %collective-permute-start.1 = (bf16[512,2048]{1,0:T(8,128)(2,1)S(1)}, bf16[512,2048]{1,0:T(8,128)(2,1)S(1)}, u32[]{:S(2)}, u32[]{:S(2)}) collective-permute-start(bf16[512,2048]{1,0:T(8,128)(2,1)S(1)} %get-tuple-element.39), channel_id=1, source_target_pairs={{0,4},{4,0},{1,5},{5,1},{2,6},{6,2},{3,7},{7,3},{8,12},{12,8},{9,1... | collective-permute-start | bytes 6291464 | tf_op jit(solution)/shard_map/ppermute | solution.py:64
  8.0 2.4 %shard_map.76.own_t.turned_ref = bf16[1024,512]{1,0:T(8,128)(2,1)S(1)} custom-call(s32[2,4]{1,0:T(2,128)S(1)} %copy-done.5, bf16[512,1024]{1,0:T(8,128)(2,1)S(1)} %copy-done.3), custom_call_target="tpu_custom_call" | custom-call | bytes 3145728 | tf_op jit(solution)/shard_map/pallas_call | solution.py:101
  10.4 0.1 collective-permute-start
  10.5 2.8 %collective-permute-done.other_t = bf16[1024,512]{1,0:T(8,128)(2,1)S(1)} collective-permute-done((bf16[1024,512]{1,0:T(8,128)(2,1)S(1)}, bf16[1024,512]{1,0:T(8,128)(2,1)S(1)}, u32[]{:S(2)}, u32[]{:S(2)}) %collective-permute-start) | collective-permute-done | bytes 1048608 | tf_op jit(solution)/shard_map/ppermute | solution.py:64
  13.2 4.1 %shard_map.80 = (bf16[1024,512]{1,0:T(8,128)(2,1)}, bf16[1024,512]{1,0:T(8,128)(2,1)}) custom-call(s32[4]{0:T(128)S(1)} %pad_add_fusion.at_ref, bf16[1024,512]{1,0:T(8,128)(2,1)S(1)} %shard_map.76.own_t.turned_ref, bf16[1024,512]{1,0:T(8,128)(2,1)S(1)} %collective-permute-done.other_t, bf16[512,2048]{1,0:T(8,128)(2,1)S(1)} %get-tuple-element.38.mine, ...), custom_call_target="tpu_custom_call" | custom-call | flops 2147483648 | bytes 8388608 | tf_op jit(solution)/shard_map/pallas_call | solution.py:174
  17.4 2.2 %collective-permute-start.8 = (bf16[1024,512]{1,0:T(8,128)(2,1)}, bf16[1024,512]{1,0:T(8,128)(2,1)}, u32[]{:S(2)}, u32[]{:S(2)}) collective-permute-start(bf16[1024,512]{1,0:T(8,128)(2,1)} %get-tuple-element.49), channel_id=1, source_target_pairs={{0,128},{4,36},{16,144},{20,52},{32,160},{36,4},{48,176},{52,20},{... | collective-permute-start | bytes 3145736 | tf_op jit(solution)/shard_map/ppermute | solution.py:50
  19.5 3.3 %shard_map.78 = (bf16[1024,512]{1,0:T(8,128)(2,1)}, f32[1024,512]{1,0:T(8,128)S(1)}) custom-call(s32[4]{0:T(128)S(1)} %pad_add_fusion.at_ref, bf16[1024,512]{1,0:T(8,128)(2,1)S(1)} %shard_map.76.own_t.turned_ref, bf16[1024,512]{1,0:T(8,128)(2,1)S(1)} %collective-permute-done.other_t, bf16[512,2048]{1,0:T(8,128)(2,1)S(1)} %get-tuple-element.38.mine, ...), custom_call_target="tpu_custom_call" | custom-call | flops 2147483648 | bytes 8388608 | tf_op jit(solution)/shard_map/pallas_call | solution.py:174
  22.8 1.1 collective-permute-start.9
  24.0 1.0 collective-permute-start.2
  25.0 8.7 %collective-permute-start.3 = (bf16[64,1024]{1,0:T(8,128)(2,1)S(1)}, bf16[64,1024]{1,0:T(8,128)(2,1)S(1)}, u32[]{:S(2)}, u32[]{:S(2)}) collective-permute-start(bf16[64,1024]{1,0:T(8,128)(2,1)S(1)} %copy-done.4), channel_id=1, source_target_pairs={{4,8},{8,4},{5,9},{9,5},{6,10},{10,6},{7,11},{11,7},{20,24},{24,20... | collective-permute-start | bytes 393224 | tf_op jit(solution)/shard_map/ppermute | solution.py:331
  33.7 3.8 %collective-permute-done.3 = bf16[64,1024]{1,0:T(8,128)(2,1)S(1)} collective-permute-done((bf16[64,1024]{1,0:T(8,128)(2,1)S(1)}, bf16[64,1024]{1,0:T(8,128)(2,1)S(1)}, u32[]{:S(2)}, u32[]{:S(2)}) %collective-permute-start.3) | collective-permute-done | bytes 131104 | tf_op jit(solution)/shard_map/ppermute | solution.py:331
  37.6 1.0 collective-permute-start.4
  38.5 1.8 %collective-permute-start.5 = (bf16[128,1024]{1,0:T(8,128)(2,1)S(1)}, bf16[128,1024]{1,0:T(8,128)(2,1)S(1)}, u32[]{:S(2)}, u32[]{:S(2)}) collective-permute-start(bf16[128,1024]{1,0:T(8,128)(2,1)S(1)} %pad_maximum_fusion.1), channel_id=1, source_target_pairs={{0,192},{4,52},{16,208},{20,4},{32,224},{36,20},{48,240},{52,36},{... | collective-permute-start | bytes 786440 | tf_op jit(solution)/shard_map/ppermute | solution.py:50
  40.3 0.5 shard_map.79.grad_ref
  40.8 1.0 copy-done.1
  41.8 5.0 %collective-permute-done.4 = bf16[128,1024]{1,0:T(8,128)(2,1)S(1)} collective-permute-done((bf16[128,1024]{1,0:T(8,128)(2,1)S(1)}, bf16[128,1024]{1,0:T(8,128)(2,1)S(1)}, u32[]{:S(2)}, u32[]{:S(2)}) %collective-permute-start.4) | collective-permute-done | bytes 262176 | tf_op jit(solution)/shard_map/ppermute | solution.py:50
  46.8 0.6 collective-permute-done.5
  47.4 2.6 %shard_map.81 = (f32[1024,128]{1,0:T(8,128)S(1)}, bf16[1024,128]{1,0:T(8,128)(2,1)S(1)}, bf16[1024,128]{1,0:T(8,128)(2,1)S(1)}, bf16[1024,128]{1,0:T(8,128)(2,1)S(1)}) custom-call(s32[4]{0:T(128)S(1)} %pad_add_fusion.at_ref, f32[1024,512]{1,0:T(8,128)S(1)} %get-tuple-element.47.refs_0_, bf16[1024,512]{1,0:T(8,128)(2,1)} %collective-permute-done.7.refs_1_, ...), custom_call_target="tpu_custom_call" | custom-call | bytes 6291456 | tf_op jit(solution)/shard_map/pallas_call | solution.py:196
  50.1 2.5 %collective-permute-start.11 = (bf16[1024,128]{1,0:T(8,128)(2,1)S(1)}, bf16[1024,128]{1,0:T(8,128)(2,1)S(1)}, u32[]{:S(2)}, u32[]{:S(2)}) collective-permute-start(bf16[1024,128]{1,0:T(8,128)(2,1)S(1)} %get-tuple-element.53), channel_id=1, source_target_pairs={{0,32},{4,132},{16,48},{20,148},{32,0},{36,164},{48,16},{52,180},{... | collective-permute-start | bytes 786440 | tf_op jit(solution)/shard_map/ppermute | solution.py:60
  52.6 0.9 collective-permute-start.12
  53.4 2.6 %collective-permute-start.6 = (bf16[128,1024]{1,0:T(8,128)(2,1)S(1)}, bf16[128,1024]{1,0:T(8,128)(2,1)S(1)}, u32[]{:S(2)}, u32[]{:S(2)}) collective-permute-start(bf16[128,1024]{1,0:T(8,128)(2,1)S(1)} %pad_maximum_fusion.1), channel_id=1, source_target_pairs={{0,128},{4,36},{16,144},{20,52},{32,160},{36,4},{48,176},{52,20},{... | collective-permute-start | bytes 786440 | tf_op jit(solution)/shard_map/ppermute | solution.py:50
  56.1 3.5 %collective-permute-done.10.refs_1_ = bf16[1024,128]{1,0:T(8,128)(2,1)S(1)} collective-permute-done((bf16[1024,128]{1,0:T(8,128)(2,1)S(1)}, bf16[1024,128]{1,0:T(8,128)(2,1)S(1)}, u32[]{:S(2)}, u32[]{:S(2)}) %collective-permute-start.10) | collective-permute-done | bytes 262176 | tf_op jit(solution)/shard_map/ppermute | solution.py:60
  59.6 0.6 collective-permute-done.12.refs_3_
  60.2 0.8 shard_map.82
  61.0 2.4 %collective-permute-done.6 = bf16[128,1024]{1,0:T(8,128)(2,1)S(1)} collective-permute-done((bf16[128,1024]{1,0:T(8,128)(2,1)S(1)}, bf16[128,1024]{1,0:T(8,128)(2,1)S(1)}, u32[]{:S(2)}, u32[]{:S(2)}) %collective-permute-start.6) | collective-permute-done | bytes 262176 | tf_op jit(solution)/shard_map/ppermute | solution.py:50
  63.4 0.1 pad_maximum_fusion.refs_0_
  63.5 0.5 collective-permute-start.13
  64.0 1.2 %collective-permute-start.14 = (bf16[4,128,1024]{2,1,0:T(8,128)(2,1)S(1)}, bf16[4,128,1024]{2,1,0:T(8,128)(2,1)}, u32[]{:S(2)}, u32[]{:S(2)}) collective-permute-start(bf16[4,128,1024]{2,1,0:T(8,128)(2,1)S(1)} %pad_maximum_fusion.refs_0_), channel_id=1, source_target_pairs={{0,32},{4,132},{16,48},{20,148},{32,0},{36,164},{48,16},{52,180},{... | collective-permute-start | bytes 3145736 | tf_op jit(solution)/shard_map/ppermute | solution.py:60
  65.2 2.0 %collective-permute-start.15 = (bf16[4,128,1024]{2,1,0:T(8,128)(2,1)S(1)}, bf16[4,128,1024]{2,1,0:T(8,128)(2,1)}, u32[]{:S(2)}, u32[]{:S(2)}) collective-permute-start(bf16[4,128,1024]{2,1,0:T(8,128)(2,1)S(1)} %pad_maximum_fusion.refs_0_), channel_id=1, source_target_pairs={{0,48},{4,196},{16,0},{20,212},{32,16},{36,228},{48,32},{52,244},{... | collective-permute-start | bytes 3145736 | tf_op jit(solution)/shard_map/ppermute | solution.py:60
  67.2 5.7 %collective-permute-start.16 = (bf16[64,1024]{1,0:T(8,128)(2,1)S(1)}, bf16[64,1024]{1,0:T(8,128)(2,1)S(1)}, u32[]{:S(2)}, u32[]{:S(2)}) collective-permute-start(bf16[64,1024]{1,0:T(8,128)(2,1)S(1)} %get-tuple-element.55), channel_id=1, source_target_pairs={{0,4},{4,12},{8,0},{12,8},{1,5},{5,13},{9,1},{13,9},{2,6},{6,14},{... | collective-permute-start | bytes 393224 | tf_op jit(solution)/shard_map/ppermute | solution.py:345
  72.9 6.7 %collective-permute-start.17 = (bf16[64,1024]{1,0:T(8,128)(2,1)S(1)}, bf16[64,1024]{1,0:T(8,128)(2,1)S(1)}, u32[]{:S(2)}, u32[]{:S(2)}) collective-permute-start(bf16[64,1024]{1,0:T(8,128)(2,1)S(1)} %get-tuple-element.61), channel_id=1, source_target_pairs={{8,4},{4,8},{9,5},{5,9},{10,6},{6,10},{11,7},{7,11},{24,20},{20,24... | collective-permute-start | bytes 393224 | tf_op jit(solution)/shard_map/ppermute | solution.py:346
  79.6 3.6 %collective-permute-done.17.p_in = bf16[64,1024]{1,0:T(8,128)(2,1)S(1)} collective-permute-done((bf16[64,1024]{1,0:T(8,128)(2,1)S(1)}, bf16[64,1024]{1,0:T(8,128)(2,1)S(1)}, u32[]{:S(2)}, u32[]{:S(2)}) %collective-permute-start.17) | collective-permute-done | bytes 131104 | tf_op jit(solution)/shard_map/ppermute | solution.py:346
  83.2 0.1 shard_map.83
  83.3 2.5 %psum.7 = f32[8,128]{1,0:T(8,128)S(1)} all-reduce(f32[8,128]{1,0:T(8,128)S(1)} %get-tuple-element.62), channel_id=1, replica_groups=mesh['x'=4,'y'=4,'zh'=2,'c'=2,'mp'=4] {'c'}, use_global_device_ids=true, to_apply=%region_0.1 | all-reduce | flops 1024 | bytes 8192 | tf_op jit(solution)/shard_map/psum | solution.py:354
  85.8 0.6 broadcast_in_dim.4
  86.4 6.8 %all-to-all-start = ((f32[8,8,128]{2,1,0:T(8,128)}), f32[8,8,128]{2,1,0:T(8,128)S(1)}, u32[]{:S(2)}, u32[]{:S(2)}) async-start(f32[8,8,128]{2,1,0:T(8,128)} %broadcast_in_dim.4), calls=%async_computation | async-start | bytes 65536 | tf_op jit(solution)/shard_map/all_to_all | solution.py:245
  93.2 0.6 collective-permute-start.18
  93.8 6.3 %all-to-all-done = f32[8,8,128]{2,1,0:T(8,128)S(1)} async-done(((f32[8,8,128]{2,1,0:T(8,128)}), f32[8,8,128]{2,1,0:T(8,128)S(1)}, u32[]{:S(2)}, u32[]{:S(2)}) %all-to-all-start) | async-done | bytes 32800 | tf_op jit(solution)/shard_map/all_to_all | solution.py:245
  100.1 1.8 %collective-permute-start.19 = (bf16[4,128,1024]{2,1,0:T(8,128)(2,1)}, bf16[4,128,1024]{2,1,0:T(8,128)(2,1)}, u32[]{:S(2)}, u32[]{:S(2)}) collective-permute-start(bf16[4,128,1024]{2,1,0:T(8,128)(2,1)} %collective-permute-done.13.refs_1_), channel_id=1, source_target_pairs={{0,4},{4,0},{1,5},{5,1},{2,6},{6,2},{3,7},{7,3},{8,12},{12,8},{9,1... | collective-permute-start | bytes 3145736 | tf_op jit(solution)/shard_map/ppermute | solution.py:64
  102.0 0.1 collective-permute-start.20
  102.1 0.4 collective-permute-start.21
  102.5 0.6 broadcast_in_dim.5
  103.1 3.9 %all-to-all-start.1 = ((f32[16,8,128]{2,1,0:T(8,128)}), f32[16,8,128]{2,1,0:T(8,128)S(1)}, u32[]{:S(2)}, u32[]{:S(2)}) async-start(f32[16,8,128]{2,1,0:T(8,128)} %broadcast_in_dim.5), calls=%async_computation.1 | async-start | bytes 131072 | tf_op jit(solution)/shard_map/all_to_all | solution.py:245
  107.1 0.5 collective-permute-done.21.refs_7_
  107.6 9.0 %shard_map.84 = bf16[512,4096]{1,0:T(8,128)(2,1)} custom-call(s32[4]{0:T(128)S(1)} %pad_add_fusion.at_ref, bf16[512,1024]{1,0:T(8,128)(2,1)S(1)} %copy-done.2, bf16[4,128,1024]{2,1,0:T(8,128)(2,1)S(1)} %pad_maximum_fusion.refs_0_, bf16[4,128,1024]{2,1,0:T(8,128)(2,1)} %collective-permute-done.13.refs_1_, ...), custom_call_target="tpu_custom_call" | custom-call | flops 4294967296 | bytes 13631488 | tf_op jit(solution)/shard_map/pallas_call | solution.py:298
  116.6 0.9 shard_map.85
  (33 shorter events, 0.3 us)
Async XLA Ops:
  0.7 2.2 %copy-start = (bf16[512,4096]{1,0:T(8,128)(2,1)S(1)}, bf16[512,4096]{1,0:T(8,128)(2,1)}, u32[]{:S(2)}) copy-start(bf16[512,4096]{1,0:T(8,128)(2,1)} %hidden_ref.1) | copy-start | bytes 12582916
  2.9 5.0 %copy-start.3 = (bf16[512,1024]{1,0:T(8,128)(2,1)S(1)}, bf16[512,1024]{1,0:T(8,128)(2,1)}, u32[]{:S(2)}) copy-start(bf16[512,1024]{1,0:T(8,128)(2,1)} %cot_ref.1) | copy-start | bytes 3145732
  2.9 5.0 %copy-start.5 = (s32[2,4]{1,0:T(2,128)S(1)}, s32[2,4]{1,0:T(2,128)}, u32[]{:S(2)}) copy-start(s32[2,4]{1,0:T(2,128)} %len_ref.1) | copy-start | bytes 100
  4.6 8.6 %collective-permute-start.1 = (bf16[512,2048]{1,0:T(8,128)(2,1)S(1)}, bf16[512,2048]{1,0:T(8,128)(2,1)S(1)}, u32[]{:S(2)}, u32[]{:S(2)}) collective-permute-start(bf16[512,2048]{1,0:T(8,128)(2,1)S(1)} %get-tuple-element.39), channel_id=1, source_target_pairs={{0,4},{4,0},{1,5},{5,1},{2,6},{6,2},{3,7},{7,3},{8,12},{12,8},{9,1... | collective-permute-start | bytes 6291464 | tf_op jit(solution)/shard_map/ppermute | solution.py:64
  10.4 2.9 %collective-permute-start = (bf16[1024,512]{1,0:T(8,128)(2,1)S(1)}, bf16[1024,512]{1,0:T(8,128)(2,1)S(1)}, u32[]{:S(2)}, u32[]{:S(2)}) collective-permute-start(bf16[1024,512]{1,0:T(8,128)(2,1)S(1)} %shard_map.76.own_t.turned_ref), channel_id=1, source_target_pairs={{0,4},{4,0},{1,5},{5,1},{2,6},{6,2},{3,7},{7,3},{8,12},{12,8},{9,1... | collective-permute-start | bytes 3145736 | tf_op jit(solution)/shard_map/ppermute | solution.py:64
  17.4 30.0 %collective-permute-start.7 = (bf16[1024,512]{1,0:T(8,128)(2,1)}, bf16[1024,512]{1,0:T(8,128)(2,1)}, u32[]{:S(2)}, u32[]{:S(2)}) collective-permute-start(bf16[1024,512]{1,0:T(8,128)(2,1)} %get-tuple-element.48), channel_id=1, source_target_pairs={{0,64},{4,20},{16,80},{20,36},{32,96},{36,52},{48,112},{52,4},{64,... | collective-permute-start | bytes 3145736 | tf_op jit(solution)/shard_map/ppermute | solution.py:50
  17.4 6.6 %copy-start.4 = (bf16[64,1024]{1,0:T(8,128)(2,1)S(1)}, bf16[64,1024]{1,0:T(8,128)(2,1)}, u32[]{:S(2)}) copy-start(bf16[64,1024]{1,0:T(8,128)(2,1)} %weight.1) | copy-start | bytes 393220
  17.4 30.0 %collective-permute-start.8 = (bf16[1024,512]{1,0:T(8,128)(2,1)}, bf16[1024,512]{1,0:T(8,128)(2,1)}, u32[]{:S(2)}, u32[]{:S(2)}) collective-permute-start(bf16[1024,512]{1,0:T(8,128)(2,1)} %get-tuple-element.49), channel_id=1, source_target_pairs={{0,128},{4,36},{16,144},{20,52},{32,160},{36,4},{48,176},{52,20},{... | collective-permute-start | bytes 3145736 | tf_op jit(solution)/shard_map/ppermute | solution.py:50
  22.8 24.6 %collective-permute-start.9 = (bf16[1024,512]{1,0:T(8,128)(2,1)}, bf16[1024,512]{1,0:T(8,128)(2,1)}, u32[]{:S(2)}, u32[]{:S(2)}) collective-permute-start(bf16[1024,512]{1,0:T(8,128)(2,1)} %get-tuple-element.50), channel_id=1, source_target_pairs={{0,192},{4,52},{16,208},{20,4},{32,224},{36,20},{48,240},{52,36},{... | collective-permute-start | bytes 3145736 | tf_op jit(solution)/shard_map/ppermute | solution.py:50
  24.0 9.7 %collective-permute-start.2 = (bf16[64,1024]{1,0:T(8,128)(2,1)S(1)}, bf16[64,1024]{1,0:T(8,128)(2,1)S(1)}, u32[]{:S(2)}, u32[]{:S(2)}) collective-permute-start(bf16[64,1024]{1,0:T(8,128)(2,1)S(1)} %copy-done.4), channel_id=1, source_target_pairs={{0,8},{4,0},{8,12},{12,4},{1,9},{5,1},{9,13},{13,5},{2,10},{6,2},{... | collective-permute-start | bytes 393224 | tf_op jit(solution)/shard_map/ppermute | solution.py:330
  25.0 12.5 %collective-permute-start.3 = (bf16[64,1024]{1,0:T(8,128)(2,1)S(1)}, bf16[64,1024]{1,0:T(8,128)(2,1)S(1)}, u32[]{:S(2)}, u32[]{:S(2)}) collective-permute-start(bf16[64,1024]{1,0:T(8,128)(2,1)S(1)} %copy-done.4), channel_id=1, source_target_pairs={{4,8},{8,4},{5,9},{9,5},{6,10},{10,6},{7,11},{11,7},{20,24},{24,20... | collective-permute-start | bytes 393224 | tf_op jit(solution)/shard_map/ppermute | solution.py:331
  37.6 9.2 %collective-permute-start.4 = (bf16[128,1024]{1,0:T(8,128)(2,1)S(1)}, bf16[128,1024]{1,0:T(8,128)(2,1)S(1)}, u32[]{:S(2)}, u32[]{:S(2)}) collective-permute-start(bf16[128,1024]{1,0:T(8,128)(2,1)S(1)} %pad_maximum_fusion.1), channel_id=1, source_target_pairs={{0,64},{4,20},{16,80},{20,36},{32,96},{36,52},{48,112},{52,4},{64,... | collective-permute-start | bytes 786440 | tf_op jit(solution)/shard_map/ppermute | solution.py:50
  38.5 8.9 %collective-permute-start.5 = (bf16[128,1024]{1,0:T(8,128)(2,1)S(1)}, bf16[128,1024]{1,0:T(8,128)(2,1)S(1)}, u32[]{:S(2)}, u32[]{:S(2)}) collective-permute-start(bf16[128,1024]{1,0:T(8,128)(2,1)S(1)} %pad_maximum_fusion.1), channel_id=1, source_target_pairs={{0,192},{4,52},{16,208},{20,4},{32,224},{36,20},{48,240},{52,36},{... | collective-permute-start | bytes 786440 | tf_op jit(solution)/shard_map/ppermute | solution.py:50
  40.8 1.0 copy-start.1
  50.0 9.6 %collective-permute-start.10 = (bf16[1024,128]{1,0:T(8,128)(2,1)S(1)}, bf16[1024,128]{1,0:T(8,128)(2,1)S(1)}, u32[]{:S(2)}, u32[]{:S(2)}) collective-permute-start(bf16[1024,128]{1,0:T(8,128)(2,1)S(1)} %get-tuple-element.52), channel_id=1, source_target_pairs={{0,16},{4,68},{16,32},{20,84},{32,48},{36,100},{48,0},{52,116},{64... | collective-permute-start | bytes 786440 | tf_op jit(solution)/shard_map/ppermute | solution.py:60
  50.1 9.5 %collective-permute-start.11 = (bf16[1024,128]{1,0:T(8,128)(2,1)S(1)}, bf16[1024,128]{1,0:T(8,128)(2,1)S(1)}, u32[]{:S(2)}, u32[]{:S(2)}) collective-permute-start(bf16[1024,128]{1,0:T(8,128)(2,1)S(1)} %get-tuple-element.53), channel_id=1, source_target_pairs={{0,32},{4,132},{16,48},{20,148},{32,0},{36,164},{48,16},{52,180},{... | collective-permute-start | bytes 786440 | tf_op jit(solution)/shard_map/ppermute | solution.py:60
  52.6 7.6 %collective-permute-start.12 = (bf16[1024,128]{1,0:T(8,128)(2,1)S(1)}, bf16[1024,128]{1,0:T(8,128)(2,1)S(1)}, u32[]{:S(2)}, u32[]{:S(2)}) collective-permute-start(bf16[1024,128]{1,0:T(8,128)(2,1)S(1)} %get-tuple-element.54), channel_id=1, source_target_pairs={{0,48},{4,196},{16,0},{20,212},{32,16},{36,228},{48,32},{52,244},{... | collective-permute-start | bytes 786440 | tf_op jit(solution)/shard_map/ppermute | solution.py:60
  53.4 9.9 %collective-permute-start.6 = (bf16[128,1024]{1,0:T(8,128)(2,1)S(1)}, bf16[128,1024]{1,0:T(8,128)(2,1)S(1)}, u32[]{:S(2)}, u32[]{:S(2)}) collective-permute-start(bf16[128,1024]{1,0:T(8,128)(2,1)S(1)} %pad_maximum_fusion.1), channel_id=1, source_target_pairs={{0,128},{4,36},{16,144},{20,52},{32,160},{36,4},{48,176},{52,20},{... | collective-permute-start | bytes 786440 | tf_op jit(solution)/shard_map/ppermute | solution.py:50
  60.2 47.4 %copy-start.2 = (bf16[512,1024]{1,0:T(8,128)(2,1)S(1)}, bf16[512,1024]{1,0:T(8,128)(2,1)}, u32[]{:S(2)}) copy-start(bf16[512,1024]{1,0:T(8,128)(2,1)} %copy-done.1) | copy-start | bytes 3145732
  63.5 36.6 %collective-permute-start.13 = (bf16[4,128,1024]{2,1,0:T(8,128)(2,1)S(1)}, bf16[4,128,1024]{2,1,0:T(8,128)(2,1)}, u32[]{:S(2)}, u32[]{:S(2)}) collective-permute-start(bf16[4,128,1024]{2,1,0:T(8,128)(2,1)S(1)} %pad_maximum_fusion.refs_0_), channel_id=1, source_target_pairs={{0,16},{4,68},{16,32},{20,84},{32,48},{36,100},{48,0},{52,116},{64... | collective-permute-start | bytes 3145736 | tf_op jit(solution)/shard_map/ppermute | solution.py:60
  64.0 36.1 %collective-permute-start.14 = (bf16[4,128,1024]{2,1,0:T(8,128)(2,1)S(1)}, bf16[4,128,1024]{2,1,0:T(8,128)(2,1)}, u32[]{:S(2)}, u32[]{:S(2)}) collective-permute-start(bf16[4,128,1024]{2,1,0:T(8,128)(2,1)S(1)} %pad_maximum_fusion.refs_0_), channel_id=1, source_target_pairs={{0,32},{4,132},{16,48},{20,148},{32,0},{36,164},{48,16},{52,180},{... | collective-permute-start | bytes 3145736 | tf_op jit(solution)/shard_map/ppermute | solution.py:60
  65.2 34.9 %collective-permute-start.15 = (bf16[4,128,1024]{2,1,0:T(8,128)(2,1)S(1)}, bf16[4,128,1024]{2,1,0:T(8,128)(2,1)}, u32[]{:S(2)}, u32[]{:S(2)}) collective-permute-start(bf16[4,128,1024]{2,1,0:T(8,128)(2,1)S(1)} %pad_maximum_fusion.refs_0_), channel_id=1, source_target_pairs={{0,48},{4,196},{16,0},{20,212},{32,16},{36,228},{48,32},{52,244},{... | collective-permute-start | bytes 3145736 | tf_op jit(solution)/shard_map/ppermute | solution.py:60
  67.2 12.4 %collective-permute-start.16 = (bf16[64,1024]{1,0:T(8,128)(2,1)S(1)}, bf16[64,1024]{1,0:T(8,128)(2,1)S(1)}, u32[]{:S(2)}, u32[]{:S(2)}) collective-permute-start(bf16[64,1024]{1,0:T(8,128)(2,1)S(1)} %get-tuple-element.55), channel_id=1, source_target_pairs={{0,4},{4,12},{8,0},{12,8},{1,5},{5,13},{9,1},{13,9},{2,6},{6,14},{... | collective-permute-start | bytes 393224 | tf_op jit(solution)/shard_map/ppermute | solution.py:345
  72.9 10.3 %collective-permute-start.17 = (bf16[64,1024]{1,0:T(8,128)(2,1)S(1)}, bf16[64,1024]{1,0:T(8,128)(2,1)S(1)}, u32[]{:S(2)}, u32[]{:S(2)}) collective-permute-start(bf16[64,1024]{1,0:T(8,128)(2,1)S(1)} %get-tuple-element.61), channel_id=1, source_target_pairs={{8,4},{4,8},{9,5},{5,9},{10,6},{6,10},{11,7},{7,11},{24,20},{20,24... | collective-permute-start | bytes 393224 | tf_op jit(solution)/shard_map/ppermute | solution.py:346
  86.4 13.7 %all-to-all-start = ((f32[8,8,128]{2,1,0:T(8,128)}), f32[8,8,128]{2,1,0:T(8,128)S(1)}, u32[]{:S(2)}, u32[]{:S(2)}) async-start(f32[8,8,128]{2,1,0:T(8,128)} %broadcast_in_dim.4), calls=%async_computation | async-start | bytes 65536 | tf_op jit(solution)/shard_map/all_to_all | solution.py:245
  93.2 13.9 %collective-permute-start.18 = (bf16[4,128,1024]{2,1,0:T(8,128)(2,1)S(1)}, bf16[4,128,1024]{2,1,0:T(8,128)(2,1)}, u32[]{:S(2)}, u32[]{:S(2)}) collective-permute-start(bf16[4,128,1024]{2,1,0:T(8,128)(2,1)S(1)} %pad_maximum_fusion.refs_0_), channel_id=1, source_target_pairs={{0,4},{4,0},{1,5},{5,1},{2,6},{6,2},{3,7},{7,3},{8,12},{12,8},{9,1... | collective-permute-start | bytes 3145736 | tf_op jit(solution)/shard_map/ppermute | solution.py:64
  100.1 6.9 %collective-permute-start.19 = (bf16[4,128,1024]{2,1,0:T(8,128)(2,1)}, bf16[4,128,1024]{2,1,0:T(8,128)(2,1)}, u32[]{:S(2)}, u32[]{:S(2)}) collective-permute-start(bf16[4,128,1024]{2,1,0:T(8,128)(2,1)} %collective-permute-done.13.refs_1_), channel_id=1, source_target_pairs={{0,4},{4,0},{1,5},{5,1},{2,6},{6,2},{3,7},{7,3},{8,12},{12,8},{9,1... | collective-permute-start | bytes 3145736 | tf_op jit(solution)/shard_map/ppermute | solution.py:64
  102.0 5.1 %collective-permute-start.20 = (bf16[4,128,1024]{2,1,0:T(8,128)(2,1)}, bf16[4,128,1024]{2,1,0:T(8,128)(2,1)}, u32[]{:S(2)}, u32[]{:S(2)}) collective-permute-start(bf16[4,128,1024]{2,1,0:T(8,128)(2,1)} %collective-permute-done.14.refs_2_), channel_id=1, source_target_pairs={{0,4},{4,0},{1,5},{5,1},{2,6},{6,2},{3,7},{7,3},{8,12},{12,8},{9,1... | collective-permute-start | bytes 3145736 | tf_op jit(solution)/shard_map/ppermute | solution.py:64
  102.1 5.5 %collective-permute-start.21 = (bf16[4,128,1024]{2,1,0:T(8,128)(2,1)}, bf16[4,128,1024]{2,1,0:T(8,128)(2,1)}, u32[]{:S(2)}, u32[]{:S(2)}) collective-permute-start(bf16[4,128,1024]{2,1,0:T(8,128)(2,1)} %collective-permute-done.15.refs_3_), channel_id=1, source_target_pairs={{0,4},{4,0},{1,5},{5,1},{2,6},{6,2},{3,7},{7,3},{8,12},{12,8},{9,1... | collective-permute-start | bytes 3145736 | tf_op jit(solution)/shard_map/ppermute | solution.py:64
  103.1 13.5 %all-to-all-start.1 = ((f32[16,8,128]{2,1,0:T(8,128)}), f32[16,8,128]{2,1,0:T(8,128)S(1)}, u32[]{:S(2)}, u32[]{:S(2)}) async-start(f32[16,8,128]{2,1,0:T(8,128)} %broadcast_in_dim.5), calls=%async_computation.1 | async-start | bytes 131072 | tf_op jit(solution)/shard_map/all_to_all | solution.py:245
  107.0 9.6 %copy-start.6 = (f32[64]{0:T(128)S(1)}, f32[64]{0:T(128)}, u32[]{:S(2)}) copy-start(f32[64]{0:T(128)} %param.7) | copy-start | bytes 772
